TPU v7x, 256 devices: a whole 4x4x8 slice. The times are simulated.
256 devices in a mesh: pair: 4 (over y), value: 64 (over z, x, core).
Axes of the slice: x: 4, y: 4, z: 8, core: 2. Of those that a mesh axis runs over, the one named last changes fastest.
Arguments:
- student: bfloat16 [1536, 65536], P('pair', 'value'), may hold values from -8 to 8
- teacher: bfloat16 [1536, 65536], P('pair', 'value'), may hold values from -8 to 8
- bw_table: float32 [8], replicated, may hold values from 0.5 to 8
- bw_index: int32 [4], replicated, may hold values from 0 to 7
- group_ids: int32 [1536], replicated, may hold values from 0 to 15, as said below
Outputs:
- force: float32 [1536, 65536], P('pair', 'value')
- loss: float32 [], replicated
Inputs may be any that keep to these rules, and one draw needn't show every extreme that they name: `group_ids`: every group from 0 to 15 holds at least one sample.
All inputs are finite; a program needn't handle non-finite values.
Results may differ from a plain program's by a relative error of at most 0.00045.
The roundings to bfloat16 on the way count: a program that leaves them out, or rounds other values in their place, can miss the bound.
Values may be sent and summed in bfloat16 or wider, within the bound.
A program may use at most 64 MiB of HBM per device.

v0:
```python
import jax.numpy as jnp

LATENT = 65536
SAMPLES = 1536


def kernel_terms(
    gram_self, gram_cross, norm_rows, norm_student, norm_teacher, same_group, heights, latent
):
    dist_self = jnp.maximum(norm_rows[:, None] + norm_student[None, :] - 2.0 * gram_self, 0.0)
    dist_cross = jnp.maximum(norm_rows[:, None] + norm_teacher[None, :] - 2.0 * gram_cross, 0.0)
    kern_self = jnp.zeros_like(dist_self)
    kern_cross = jnp.zeros_like(dist_cross)
    weight_self = jnp.zeros_like(dist_self)
    weight_cross = jnp.zeros_like(dist_cross)
    count = heights.shape[0]
    for member in range(count):
        height = heights[member]
        width_now = height * latent
        exp_self = jnp.exp(-dist_self / width_now)
        exp_cross = jnp.exp(-dist_cross / width_now)
        kern_self = kern_self + exp_self
        kern_cross = kern_cross + exp_cross
        weight_self = weight_self + exp_self / height
        weight_cross = weight_cross + exp_cross / height
    kern_self = kern_self / count * same_group
    kern_cross = kern_cross / count * same_group
    weight_self = weight_self / count * same_group
    weight_cross = weight_cross / count * same_group
    row_loss = jnp.sum(kern_self - 2.0 * kern_cross, axis=1)
    total_self = jnp.sum(weight_self, axis=1)
    total_cross = jnp.sum(weight_cross, axis=1)
    return (
        weight_self.astype(jnp.bfloat16),
        weight_cross.astype(jnp.bfloat16),
        row_loss,
        total_self,
        total_cross,
    )


def reference(student, teacher, bw_table, bw_index, group_ids):
    student_wide = student.astype(jnp.float32)
    teacher_wide = teacher.astype(jnp.float32)
    norm_student = jnp.sum(student_wide * student_wide, axis=1)
    norm_teacher = jnp.sum(teacher_wide * teacher_wide, axis=1)
    gram_self = jnp.dot(student, student.T, preferred_element_type=jnp.float32)
    gram_cross = jnp.dot(student, teacher.T, preferred_element_type=jnp.float32)
    heights = bw_table[bw_index]
    same_group = (group_ids[:, None] == group_ids[None, :]).astype(jnp.float32)
    group_sizes = jnp.sum(same_group, axis=1)
    weight_self, weight_cross, row_loss, total_self, total_cross = kernel_terms(
        gram_self,
        gram_cross,
        norm_student,
        norm_student,
        norm_teacher,
        same_group,
        heights,
        float(LATENT),
    )
    loss = jnp.sum(row_loss / group_sizes) / SAMPLES
    pulled = student_wide * (total_cross - total_self)[:, None]
    pulled = pulled + jnp.dot(weight_self, student, preferred_element_type=jnp.float32)
    pulled = pulled - jnp.dot(weight_cross, teacher, preferred_element_type=jnp.float32)
    force = pulled / group_sizes[:, None]
    return (force, loss)


def solution(mesh):
    return reference
```

profile of v0, /device:TPU:1, one launch (start us, length us, event | category | flops | bytes accessed | tf_op | source)
XLA Modules:
  0.0 334.7 jit_solution(5987754802952657437)
XLA Ops:
  7.2 0.7 all-gather.12.cloned.1.call-update
  7.9 0.0 all-gather.14.cloned.1.call-start
  8.0 0.7 all-gather.14.cloned.1.call-update
  8.7 0.0 all-reduce.9.cloned.1.call-start
  8.7 47.1 %all-gather.12.cloned.1.call-done = bf16[1536,1024]{1,0:T(8,128)(2,1)} async-done(((bf16[384,1024]{1,0:T(8,128)(2,1)}), bf16[1536,1024]{1,0:T(8,128)(2,1)}) %all-gather.12.cloned.1.call-update) | async-done | bytes 3145744 | tf_op args[1]
  55.8 4.9 %fusion.14 = f32[384,1536]{1,0:T(8,128)} fusion(bf16[384,1024]{1,0:T(8,128)(2,1)} %param, bf16[1536,1024]{1,0:T(8,128)(2,1)} %all-gather.12.cloned.1.call-done), kind=kOutput, calls=%fused_computation.36 | convolution fusion | flops 1207959552 | bytes 6291456 | tf_op jit(solution)/dot_general | solution.py:48
  60.7 39.2 %all-gather.14.cloned.1.call-done = bf16[1536,1024]{1,0:T(8,128)(2,1)} async-done(((bf16[384,1024]{1,0:T(8,128)(2,1)}), bf16[1536,1024]{1,0:T(8,128)(2,1)}) %all-gather.14.cloned.1.call-update) | async-done | bytes 3145744 | tf_op jit(solution)/dot_general | solution.py:47
  99.9 4.8 %fusion.15 = f32[384,1536]{1,0:T(8,128)} fusion(bf16[384,1024]{1,0:T(8,128)(2,1)S(1)} %copy-done.2, bf16[1536,1024]{1,0:T(8,128)(2,1)} %all-gather.14.cloned.1.call-done), kind=kOutput, calls=%fused_computation.37 | convolution fusion | flops 1207959552 | bytes 6291456 | tf_op jit(solution)/dot_general | solution.py:47
  104.8 0.6 copy-done.5
  105.4 0.6 gather_fusion
  106.1 0.7 fusion.13
  109.2 0.2 fusion.4
  109.4 0.2 multiply_reduce_fusion
  109.7 124.7 %all-reduce.5 = (f32[384]{0:T(512)S(1)}, f32[384]{0:T(512)S(1)}) all-reduce(f32[384]{0:T(512)S(1)} %fusion.4, f32[384]{0:T(512)S(1)} %multiply_reduce_fusion), channel_id=1, replica_groups=mesh['pair'=4,'value'=64] {'value'}, use_global_device_ids=true, to_apply=%region_0.0.clone | all-reduce | flops 768 | bytes 6144 | tf_op jit(solution)/reduce_sum | solution.py:45
  234.4 8.8 %all-gather.8 = f32[4,1,384]{2,1,0:T(1,128)S(1)} all-gather(f32[1,1,384]{2,1,0:T(1,128)S(1)} %reshape.48), channel_id=6, replica_groups=mesh['pair'=4,'value'=64] {'pair'}, dimensions={0}, use_global_device_ids=true | all-gather | bytes 7680 | tf_op jit(solution)/reduce_sum | solution.py:45
  243.2 8.1 %all-gather.7 = f32[4,1,384]{2,1,0:T(1,128)S(1)} all-gather(f32[1,1,384]{2,1,0:T(1,128)S(1)} %reshape.46), channel_id=3, replica_groups=mesh['pair'=4,'value'=64] {'pair'}, dimensions={0}, use_global_device_ids=true | all-gather | bytes 7680 | tf_op jit(solution)/reduce_sum | solution.py:46
  251.3 0.6 dynamic-slice
  252.6 0.1 dynamic-slice.2
  252.7 47.4 %all-reduce.9.cloned.1.call-done = (f32[384,1536]{1,0:T(8,128)}, f32[384,1536]{1,0:T(8,128)}) async-done(((f32[384,1536]{1,0:T(8,128)}, f32[384,1536]{1,0:T(8,128)}), (f32[384,1536]{1,0:T(8,128)}, f32[384,1536]{1,0:T(8,128)})) %all-reduce.9.cloned.1.call-update) | async-done | bytes 4718608 | tf_op jit(solution)/dot_general | solution.py:47
  300.0 10.6 %fusion.2 = (f32[384]{0:T(512)S(1)}, f32[384]{0:T(512)S(1)}, f32[384]{0:T(512)S(1)}, bf16[384,1536]{1,0:T(8,128)(2,1)S(1)}, f32[384]{0:T(512)S(1)}, /*index=5*/bf16[384,1536]{1,0:T(8,128)(2,1)S(1)}) fusion(s32[1536]{0:T(1024)S(1)} %copy-done.3, s32[384]{0:T(512)S(1)} %dynamic-slice.2, f32[]{:T(128)S(6)} %mul.52, f32[]{:T(128)S(6)} %mul.53, f32[]{:T(128)S(6)} %mul.54, ...), kind=kLoop, calls=%fused_computation.8 | loop fusion | flops 33028608 | bytes 7105568 | tf_op jit(solution)/reduce_sum | solution.py:30
  310.6 0.6 divide_reduce_fusion
  311.2 9.1 %all-reduce.4 = f32[]{:T(128)} all-reduce(f32[]{:T(128)} %divide_reduce_fusion), channel_id=12, replica_groups=mesh['pair'=4,'value'=64] {'pair'}, use_global_device_ids=true, to_apply=%region_6.0.clone | all-reduce | flops 1 | bytes 8 | tf_op jit(solution)/reduce_sum | solution.py:62
  320.9 3.4 %fusion.9 = f32[384,1024]{1,0:T(8,128)S(1)} fusion(bf16[1536,1024]{1,0:T(8,128)(2,1)} %all-gather.14.cloned.1.call-done, bf16[384,1536]{1,0:T(8,128)(2,1)S(1)} %get-tuple-element.11), kind=kOutput, calls=%fused_computation.28 | convolution fusion | flops 1207959552 | bytes 5898240 | tf_op jit(solution)/dot_general | solution.py:64
  324.4 2.7 fusion.7
  (24 shorter events, 0.2 us)
Async XLA Ops:
  7.2 98.2 %copy-start = (f32[8]{0:T(128)S(1)}, f32[8]{0:T(128)}, u32[]{:S(2)}) copy-start(f32[8]{0:T(128)} %param.3) | copy-start | bytes 100
  7.2 48.6 %all-gather.12.cloned.1.call-start = ((), (), s32[]{:S(2)}) async-start(), calls=%async_computation | async-start | bytes 3932160 | tf_op args[1]
  7.9 92.0 %all-gather.14.cloned.1.call-start = ((), (), s32[]{:S(2)}) async-start(), calls=%async_computation.1 | async-start | bytes 3932160 | tf_op jit(solution)/dot_general | solution.py:47
  8.7 91.3 %copy-start.2 = (bf16[384,1024]{1,0:T(8,128)(2,1)S(1)}, bf16[384,1024]{1,0:T(8,128)(2,1)}, u32[]{:S(2)}) copy-start(bf16[384,1024]{1,0:T(8,128)(2,1)} %param) | copy-start | bytes 2359300
  8.7 291.4 %all-reduce.9.cloned.1.call-start = ((), (), s32[]{:S(2)}) async-start(), calls=%async_computation.2 | async-start | bytes 9437184 | tf_op jit(solution)/dot_general | solution.py:47
  104.7 0.7 copy-start.5
  104.7 4.7 %copy-start.1 = (bf16[384,1024]{1,0:T(8,128)(2,1)S(1)}, bf16[384,1024]{1,0:T(8,128)(2,1)}, u32[]{:S(2)}) copy-start(bf16[384,1024]{1,0:T(8,128)(2,1)} %param.2) | copy-start | bytes 2359300
  104.7 146.6 %copy-start.6 = (u32[256]{0:T(256)S(1)}, u32[256]{0:T(256)}, u32[]{:S(2)}) copy-start(u32[256]{0:T(256)} %constant.32) | copy-start | bytes 3076
  104.7 147.9 %copy-start.3 = (s32[1536]{0:T(1024)S(1)}, s32[1536]{0:T(1024)}, u32[]{:S(2)}) copy-start(s32[1536]{0:T(1024)} %param.1) | copy-start | bytes 18436
  320.9 3.4 %copy-start.4 = (bf16[1536,1024]{1,0:T(8,128)(2,1)S(1)}, bf16[1536,1024]{1,0:T(8,128)(2,1)}, u32[]{:S(2)}) copy-start(bf16[1536,1024]{1,0:T(8,128)(2,1)} %all-gather.12.cloned.1.call-done) | copy-start | bytes 9437188
Sparse Core Ops, SparseCore 0:
  9.8 45.9 all-gather.11
  57.6 42.3 all-gather.13
  104.9 195.1 all-reduce.8
where the time goes:
time: 338 us; the launch traced here: 335 us
  blocking collectives  151 us (45%)
  waiting for transfers between devices  135 us (40%)
  between operations  18.8 us (6%)
  matrix products  15.8 us (5%)
  other arithmetic  11.7 us (3%)
    reduce_sum x2, blocking collectives, reference(): norm_student = jnp.sum(student_wide * student_wide, axis=1)  133 us
    dot_general x2, waiting for transfers between devices, reference(): gram_self = jnp.dot(student, student.T, preferred_element_type=jnp.float32)  86.6 us
    unnamed x4, waiting for transfers between devices  48.5 us
    reduce_sum x1, other arithmetic, kernel_terms(): row_loss = jnp.sum(kern_self - 2.0 * kern_cross, axis=1)  10.6 us
    reduce_sum x1, blocking collectives, reference(): loss = jnp.sum(row_loss / group_sizes) / SAMPLES  9.06 us
    reduce_sum x1, blocking collectives, reference(): norm_teacher = jnp.sum(teacher_wide * teacher_wide, axis=1)  8.08 us
  transfers between devices with their start and end apart: 3, of which 3 were waited for; matrix products, arithmetic and copies ran while one was open for 2% of the time, Pallas kernels for 0%

commit v1 on v0

v1 whole, which is shorter than its diff:
```python
import functools

import jax
import jax.numpy as jnp
from jax import lax
from jax.experimental import pallas as pl
from jax.experimental.pallas import tpu as pltpu
from jax.sharding import PartitionSpec as P

MESH = pl.DeviceIdType.MESH
F32, BF16 = jnp.float32, jnp.bfloat16


class Sizes:
    def __init__(self, ny, nx, nz, nc, samples, tile, latent):
        self.ny, self.nx, self.nz, self.nc = ny, nx, nz, nc
        self.samples, self.tile, self.latent = samples, tile, float(latent)
        self.rows = samples // ny
        self.cols = tile // ny
        self.groups = 2 * nc * nx
        self.half = nz // 2
        self.cap = 8 * ny * self.half
        self.blocks = self.cap // 8


def pair_terms(dist_self, dist_cross, mask, heights, latent):
    kern_self = jnp.zeros_like(dist_self)
    kern_cross = jnp.zeros_like(dist_cross)
    weight_self = jnp.zeros_like(dist_self)
    weight_cross = jnp.zeros_like(dist_cross)
    count = len(heights)
    for height in heights:
        width_now = height * latent
        exp_self = jnp.exp(-dist_self / width_now)
        exp_cross = jnp.exp(-dist_cross / width_now)
        kern_self = kern_self + exp_self
        kern_cross = kern_cross + exp_cross
        weight_self = weight_self + exp_self / height
        weight_cross = weight_cross + exp_cross / height
    kern_self = kern_self / count * mask
    kern_cross = kern_cross / count * mask
    weight_self = weight_self / count * mask
    weight_cross = weight_cross / count * mask
    row_loss = jnp.sum(kern_self - 2.0 * kern_cross, axis=1, keepdims=True)
    pull = jnp.sum(weight_cross, axis=1, keepdims=True) - jnp.sum(weight_self, axis=1, keepdims=True)
    return weight_self.astype(BF16), weight_cross.astype(BF16), row_loss, pull


class Pool:
    def __init__(self):
        self.total = 0

    def take(self, count):
        first = self.total
        self.total += count
        return first

    def pair(self, count):
        return self.take(count), self.take(count)


def exchanges(z):
    pool = Pool()
    sizes = {
        "in_s": z.ny, "in_t": z.ny, "core": z.groups // 2, "a1": z.nx, "b1": z.ny, "a2": z.ny, "b2": z.nx, "z3": z.nz,
        "gz_w": z.nz, "gz_t": z.nz, "g2a_w": z.ny, "g2a_t": z.ny, "g2b_w": z.nx, "g2b_t": z.nx,
        "g1a_w": z.nx, "g1a_t": z.nx, "g1b_w": z.ny, "g1b_t": z.ny, "gc_w": 1, "gc_t": 1, "out": z.ny, "own": 3,
    }
    return {name: pool.pair(count) for name, count in sizes.items()}, pool.total


def fused(z, ids, s_ref, t_ref, gr_ref, gc_ref, tab_ref, idx_ref, f_ref, l_ref,
          xin_s, xin_t, sort_ref, back_ref, xacc, xs, d_ref, rc, r1a, r1b, sums, r2a, r2b, u_ref, r3,
          wf, t3, t2a, t2b, t1a, t1b, tall, fs, fo, sems):
    y, v = lax.axis_index("pair"), lax.axis_index("value")
    c = lax.rem(v, z.nc)
    x = lax.rem(v // z.nc, z.nx)
    zc = v // (z.nc * z.nx)
    other = 1 - c
    hg = z.groups // 2
    quarter = z.cap // z.ny

    def at(yy=None, xx=None, zz=None, cc=None):
        yy = y if yy is None else yy
        xx = x if xx is None else xx
        zz = zc if zz is None else zz
        cc = c if cc is None else cc
        return (yy, (zz * z.nx + xx) * z.nc + cc)

    def on_y(k):
        return lax.rem(y + k, z.ny)

    def on_x(k):
        return lax.rem(x + k, z.nx)

    def on_z(k):
        return lax.rem(zc + k, z.nz)

    barrier = pltpu.get_barrier_semaphore()
    peers = [at(yy=on_y(k)) for k in range(1, z.ny)] + [at(xx=on_x(k)) for k in range(1, z.nx)]
    peers += [at(zz=on_z(k)) for k in range(1, z.nz)] + [at(cc=other)]
    for peer in peers:
        pl.semaphore_signal(barrier, inc=1, device_id=peer, device_id_type=MESH)
    pl.semaphore_wait(barrier, len(peers))

    def copy(name, src, dst, send, recv, device):
        first_send, first_recv = ids[name]
        return pltpu.make_async_remote_copy(
            src_ref=src, dst_ref=dst, send_sem=sems.at[first_send + send], recv_sem=sems.at[first_recv + recv],
            device_id=device, device_id_type=MESH)

    far_first = sorted(range(1, z.ny), key=lambda k: -min(k, z.ny - k))

    def in_copy(name, ref, land, k, source, target):
        cols = pl.ds(pl.multiple_of(target * z.cols, z.cols), z.cols)
        return copy(name, ref.at[:, cols], land.at[source], k, source, at(yy=on_y(k)))

    for k in far_first:
        in_copy("in_s", s_ref, xin_s, k, y, on_y(k)).start()
        in_copy("in_t", t_ref, xin_t, k, y, on_y(k)).start()
    own_cols = pl.ds(pl.multiple_of(y * z.cols, z.cols), z.cols)
    own_s = pltpu.make_async_copy(s_ref.at[:, own_cols], xin_s.at[y], sems.at[ids["own"][0]])
    own_t = pltpu.make_async_copy(t_ref.at[:, own_cols], xin_t.at[y], sems.at[ids["own"][0] + 1])
    own_s.start()
    own_t.start()

    chunk = z.rows
    for part in range(z.ny):
        cols = pl.ds(part * chunk, chunk)
        ids_row = gr_ref[:, cols]

        def count_before(step, rank):
            first = pl.multiple_of(step * z.cap, z.cap)
            ids_col = gc_ref[pl.ds(first, z.cap), :]
            at_row = first + lax.broadcasted_iota(jnp.int32, (z.cap, chunk), 0)
            at_col = part * chunk + lax.broadcasted_iota(jnp.int32, (z.cap, chunk), 1)
            hit = jnp.where((ids_col == ids_row) & (at_row < at_col), 1, 0)
            return rank + jnp.sum(hit, axis=0, keepdims=True)

        rank = lax.fori_loop(0, z.samples // z.cap, count_before, jnp.zeros((1, chunk), jnp.int32))
        place = ids_row * z.cap + rank

        def fill_sort(step, _):
            first = pl.multiple_of(step * z.cap, z.cap)
            slot = first + lax.broadcasted_iota(jnp.int32, (z.cap, chunk), 0)
            sort_ref[part, pl.ds(first, z.cap), :] = jnp.where(slot == place, 1.0, 0.0).astype(BF16)
            return 0

        lax.fori_loop(0, z.groups, fill_sort, 0)

    own_s.wait()
    own_t.wait()

    xacc[...] = jnp.zeros_like(xacc)
    slots = z.groups * z.cap
    tall_rows = slots // 4

    def sort_from(source):
        def body(step, _):
            first = pl.multiple_of(step * tall_rows, tall_rows)
            place = sort_ref[source, pl.ds(first, tall_rows), :]
            xacc[pl.ds(first, tall_rows), 0:z.cols] += jnp.dot(place, xin_s[source], preferred_element_type=F32)
            xacc[pl.ds(first, tall_rows), z.cols:2 * z.cols] += jnp.dot(place, xin_t[source], preferred_element_type=F32)
            return 0

        lax.fori_loop(0, 4, body, 0)

    sort_from(y)
    for k in reversed(far_first):
        source = on_y(z.ny - k)
        in_copy("in_s", s_ref, xin_s, k, source, on_y(k)).wait_recv()
        in_copy("in_t", t_ref, xin_t, k, source, on_y(k)).wait_recv()
        sort_from(source)

    def distances(group):
        rows = pl.ds(pl.multiple_of(group * z.cap, z.cap), z.cap)
        both = jnp.concatenate([xacc[rows, 0:z.cols], xacc[rows, z.cols:2 * z.cols]], axis=0).astype(BF16)
        xs[group] = both
        gram = lax.dot_general(both, both, (((1,), (1,)), ((), ())), preferred_element_type=F32)
        size = 2 * z.cap
        eye = lax.broadcasted_iota(jnp.int32, (size, size), 0) == lax.broadcasted_iota(jnp.int32, (size, size), 1)
        diagonal = jnp.where(eye, gram, 0.0)
        norm_row = jnp.sum(diagonal, axis=0, keepdims=True)
        norm_col = jnp.sum(diagonal[0:z.cap], axis=1, keepdims=True)
        d_ref[group] = norm_col + norm_row - 2.0 * gram[0:z.cap]

    def core_copy(i, group):
        return copy("core", d_ref.at[group], rc.at[i], i, i, at(cc=other))

    def to_other(i, _):
        distances(other * hg + i)
        core_copy(i, other * hg + i).start()
        return 0

    lax.fori_loop(0, hg, to_other, 0)

    def a1_copy(k, source):
        return copy("a1", d_ref.at[c * hg + on_x(k)], r1a.at[source], k, source, at(xx=on_x(k)))

    def b1_copy(k, source):
        return copy("b1", d_ref.at[c * hg + z.nx + on_y(k)], r1b.at[source], k, source, at(yy=on_y(k)))

    def add_core(i):
        distances(c * hg + i)
        core_copy(i, c * hg + i).wait_recv()
        d_ref[c * hg + i] += rc[i]

    def mine(k, _):
        add_core(on_x(k))

        @pl.when(k < z.nx)
        def _():
            a1_copy(k, x).start()

        add_core(z.nx + on_y(k))

        @pl.when(k < z.nx)
        def _():
            b1_copy(k, y).start()

        return 0

    lax.fori_loop(1, z.nx + 1, mine, 0)

    total_a = d_ref[c * hg + x]
    for k in range(1, z.nx):
        source = on_x(z.nx - k)
        a1_copy(k, source).wait_recv()
        total_a = total_a + r1a[source]
    sums[0] = total_a

    def a2_copy(k, source):
        rows = pl.ds(pl.multiple_of(on_y(k) * quarter, quarter), quarter)
        return copy("a2", sums.at[0, rows], r2a.at[source], k, source, at(yy=on_y(k)))

    for k in range(1, z.ny):
        a2_copy(k, y).start()
    total_b = d_ref[c * hg + z.nx + y]
    for k in range(1, z.ny):
        source = on_y(z.ny - k)
        b1_copy(k, source).wait_recv()
        total_b = total_b + r1b[source]
    sums[1] = total_b

    def b2_copy(k, source):
        rows = pl.ds(pl.multiple_of(on_x(k) * quarter, quarter), quarter)
        return copy("b2", sums.at[1, rows], r2b.at[source], k, source, at(xx=on_x(k)))

    for k in range(1, z.nx):
        b2_copy(k, x).start()

    part_a = sums[0, pl.ds(pl.multiple_of(y * quarter, quarter), quarter), :]
    for k in range(1, z.ny):
        source = on_y(z.ny - k)
        a2_copy(k, source).wait_recv()
        part_a = part_a + r2a[source]
    u_ref[0:z.half] = part_a.reshape(z.half, 8, 2 * z.cap)
    part_b = sums[1, pl.ds(pl.multiple_of(x * quarter, quarter), quarter), :]
    for k in range(1, z.nx):
        source = on_x(z.nx - k)
        b2_copy(k, source).wait_recv()
        part_b = part_b + r2b[source]
    u_ref[z.half:2 * z.half] = part_b.reshape(z.half, 8, 2 * z.cap)

    def z3_copy(k, source):
        return copy("z3", u_ref.at[on_z(k)], r3.at[source], k, source, at(zz=on_z(k)))

    for k in range(1, z.nz):
        z3_copy(k, zc).start()

    def fill_back(step, _):
        first = pl.multiple_of(step * z.cap, z.cap)
        ids_col = gc_ref[pl.ds(first, z.cap), :]
        at_row = first + lax.broadcasted_iota(jnp.int32, (z.cap, z.samples), 0)
        at_col = lax.broadcasted_iota(jnp.int32, (z.cap, z.samples), 1)
        hit = jnp.where((ids_col == gr_ref[...]) & (at_col < at_row), 1.0, 0.0)
        rank = jnp.sum(hit, axis=1, keepdims=True).astype(jnp.int32)
        place = ids_col * z.cap + rank
        slot = lax.broadcasted_iota(jnp.int32, (z.cap, slots), 1)
        back_ref[pl.ds(first, z.cap), :] = jnp.where(slot == place, 1.0, 0.0).astype(BF16)
        return 0

    lax.fori_loop(0, z.samples // z.cap, fill_back, 0)

    dist = u_ref[zc]
    for k in range(1, z.nz):
        source = on_z(z.nz - k)
        z3_copy(k, source).wait_recv()
        dist = dist + r3[source]

    way = zc // z.half
    member = (1 - way) * x + way * y
    sub = (1 - way) * y + way * x
    group = c * hg + way * z.nx + member
    block = sub * z.half + lax.rem(zc, z.half)
    size = jnp.sum(jnp.where(gr_ref[...] == group, 1.0, 0.0), axis=1, keepdims=True)
    row_at = (block * 8 + lax.broadcasted_iota(jnp.int32, (8, z.cap), 0)).astype(F32)
    col_at = lax.broadcasted_iota(jnp.int32, (8, z.cap), 1).astype(F32)
    mask = jnp.where((row_at < size) & (col_at < size), 1.0, 0.0)
    dist = jnp.maximum(dist, 0.0)
    heights = [tab_ref[idx_ref[m]] for m in range(4)]
    weight_self, weight_cross, row_loss, pull = pair_terms(
        dist[:, 0:z.cap], dist[:, z.cap:2 * z.cap], mask, heights, z.latent)
    wf[group, block] = jnp.concatenate([weight_self.astype(F32), -weight_cross.astype(F32)], axis=0).astype(BF16)
    lane = 2 * (member * z.blocks + block)
    lanes = lax.broadcasted_iota(jnp.int32, (8, 128), 1)
    t3[zc] = jnp.where(lanes == lane, pull, 0.0) + jnp.where(lanes == lane + 1, row_loss / size, 0.0)

    def gz_copies(k, source):
        way_of = source // z.half
        group_of = c * hg + way_of * z.nx + (1 - way_of) * x + way_of * y
        block_of = ((1 - way_of) * y + way_of * x) * z.half + lax.rem(source, z.half)
        place = wf.at[group_of, block_of]
        return (copy("gz_w", place, place, k, source, at(zz=on_z(k))),
                copy("gz_t", t3.at[source], t3.at[source], k, source, at(zz=on_z(k))))

    def start(pair):
        for one in pair:
            one.start()

    def wait_recv(pair):
        for one in pair:
            one.wait_recv()

    for k in range(1, z.nz):
        start(gz_copies(k, zc))
    for k in range(1, z.nz):
        wait_recv(gz_copies(k, on_z(z.nz - k)))
    t2a[y] = jnp.sum(t3[0:z.half], axis=0)
    t2b[x] = jnp.sum(t3[z.half:2 * z.half], axis=0)

    def g2a_copies(k, source):
        place = wf.at[c * hg + x, pl.ds(source * z.half, z.half)]
        return (copy("g2a_w", place, place, k, source, at(yy=on_y(k))),
                copy("g2a_t", t2a.at[source], t2a.at[source], k, source, at(yy=on_y(k))))

    def g2b_copies(k, source):
        place = wf.at[c * hg + z.nx + y, pl.ds(source * z.half, z.half)]
        return (copy("g2b_w", place, place, k, source, at(xx=on_x(k))),
                copy("g2b_t", t2b.at[source], t2b.at[source], k, source, at(xx=on_x(k))))

    for k in range(1, z.nx):
        start(g2a_copies(k, y))
        start(g2b_copies(k, x))

    def g1a_copies(k, source):
        place = wf.at[c * hg + source]
        return (copy("g1a_w", place, place, k, source, at(xx=on_x(k))),
                copy("g1a_t", t1a.at[source], t1a.at[source], k, source, at(xx=on_x(k))))

    def g1b_copies(k, source):
        place = wf.at[c * hg + z.nx + source]
        return (copy("g1b_w", place, place, k, source, at(yy=on_y(k))),
                copy("g1b_t", t1b.at[source], t1b.at[source], k, source, at(yy=on_y(k))))

    for k in range(1, z.ny):
        wait_recv(g2a_copies(k, on_y(z.ny - k)))
    t1a[x] = jnp.sum(t2a[...], axis=0)
    for k in range(1, z.nx):
        start(g1a_copies(k, x))
    for k in range(1, z.nx):
        wait_recv(g2b_copies(k, on_x(z.nx - k)))
    t1b[y] = jnp.sum(t2b[...], axis=0)
    for k in range(1, z.ny):
        start(g1b_copies(k, y))
    for k in range(1, z.nx):
        wait_recv(g1a_copies(k, on_x(z.nx - k)))
    for k in range(1, z.ny):
        wait_recv(g1b_copies(k, on_y(z.ny - k)))
    tall[c, 0] = jnp.sum(t1a[...], axis=0)
    tall[c, 1] = jnp.sum(t1b[...], axis=0)

    def gc_copies(core):
        place = wf.at[pl.ds(core * hg, hg)]
        return (copy("gc_w", place, place, 0, 0, at(cc=other)),
                copy("gc_t", tall.at[core], tall.at[core], 0, 0, at(cc=other)))

    start(gc_copies(c))

    def force_of(g):
        tile = tall[g // hg, lax.rem(g, hg) // z.nx]
        spot = lax.broadcasted_iota(jnp.int32, (z.blocks, 8, 128), 2)
        want = 2 * (lax.rem(g, z.nx) * z.blocks + lax.broadcasted_iota(jnp.int32, (z.blocks, 8, 128), 0))
        picked = jnp.where(spot == want, jnp.broadcast_to(tile[None], (z.blocks, 8, 128)), 0.0)
        pulls = jnp.sum(picked, axis=2, keepdims=True).reshape(z.cap, 1)
        held = wf[g].astype(F32).reshape(z.blocks, 2, 8, z.cap)
        weights = jnp.concatenate(
            [held[:, 0].reshape(z.cap, z.cap), held[:, 1].reshape(z.cap, z.cap)], axis=1).astype(BF16)
        values = xs[g]
        pulled = values[0:z.cap].astype(F32) * pulls + jnp.dot(weights, values, preferred_element_type=F32)
        size_of = jnp.sum(jnp.where(gr_ref[...] == g, 1.0, 0.0), axis=1, keepdims=True)
        force = pulled / size_of
        high = force.astype(BF16)
        low = (force - high.astype(F32)).astype(BF16)
        rows = pl.ds(pl.multiple_of(g * z.cap, z.cap), z.cap)
        fs[rows, 0:z.cols] = high
        fs[rows, z.cols:2 * z.cols] = low

    def own_force(i, _):
        force_of(c * hg + i)
        return 0

    def other_force(i, _):
        force_of(other * hg + i)
        return 0

    lax.fori_loop(0, hg, own_force, 0)
    wait_recv(gc_copies(other))
    lax.fori_loop(0, hg, other_force, 0)

    odd = lax.rem(lax.broadcasted_iota(jnp.int32, (8, 128), 1), 2) == 1
    every = jnp.where(odd, tall[0, 0] + tall[0, 1] + tall[1, 0] + tall[1, 1], 0.0)
    every = jnp.sum(jnp.sum(every, axis=1, keepdims=True), axis=0, keepdims=True)
    l_ref[...] = jnp.broadcast_to(every / z.samples, l_ref.shape)

    def out_copy(k, source):
        cols = pl.ds(pl.multiple_of(source * z.cols, z.cols), z.cols)
        return copy("out", fo.at[k], f_ref.at[:, cols], k, source, at(yy=on_y(k)))

    def out_local():
        return pltpu.make_async_copy(fo.at[0], f_ref.at[:, own_cols], sems.at[ids["own"][0] + 2])

    def unsort(k):
        rows = pl.ds(pl.multiple_of(on_y(k) * z.rows, z.rows), z.rows)
        moved = jnp.dot(back_ref[rows, :], fs[...], preferred_element_type=F32)
        fo[k] = moved[:, 0:z.cols] + moved[:, z.cols:2 * z.cols]

    def send_out(step, _):
        k = step if z.ny == 2 else lax.rem(step + z.ny // 2 - 1, z.ny - 1) + 1
        if z.ny == 2:
            k = 1
        unsort(k)
        out_copy(k, y).start()
        return 0

    lax.fori_loop(0, z.ny - 1, send_out, 0)
    unsort(0)
    out_local().start()
    out_local().wait()
    for k in range(1, z.ny):
        out_copy(k, on_y(z.ny - k)).wait_recv()

    for k in range(1, z.ny):
        in_copy("in_s", s_ref, xin_s, k, y, on_y(k)).wait_send()
        in_copy("in_t", t_ref, xin_t, k, y, on_y(k)).wait_send()
        b1_copy(k, y).wait_send()
        a2_copy(k, y).wait_send()
        out_copy(k, y).wait_send()
        for one in g2a_copies(k, y) + g1b_copies(k, y):
            one.wait_send()
    for k in range(1, z.nx):
        a1_copy(k, x).wait_send()
        b2_copy(k, x).wait_send()
        for one in g2b_copies(k, x) + g1a_copies(k, x):
            one.wait_send()
    for k in range(1, z.nz):
        z3_copy(k, zc).wait_send()
        for one in gz_copies(k, zc):
            one.wait_send()
    for i in range(hg):
        core_copy(i, other * hg + i).wait_send()
    for one in gc_copies(c):
        one.wait_send()


def sorted_path(z, student, teacher, bw_table, bw_index, group_ids):
    ids, count = exchanges(z)
    slots, pair, hg = z.groups * z.cap, 2 * z.cap, z.groups // 2
    quarter = z.cap // z.ny
    vmem, smem, anywhere = (pl.BlockSpec(memory_space=m) for m in (pltpu.VMEM, pltpu.SMEM, pl.ANY))
    force, loss = pl.pallas_call(
        functools.partial(fused, z, ids),
        out_shape=(jax.ShapeDtypeStruct((z.rows, z.tile), F32), jax.ShapeDtypeStruct((8, 128), F32)),
        in_specs=[anywhere, anywhere, vmem, vmem, smem, smem],
        out_specs=(anywhere, vmem),
        scratch_shapes=[
            pltpu.VMEM((z.ny, z.rows, z.cols), BF16),
            pltpu.VMEM((z.ny, z.rows, z.cols), BF16),
            pltpu.VMEM((z.ny, slots, z.rows), BF16),
            pltpu.VMEM((z.samples, slots), BF16),
            pltpu.VMEM((slots, 2 * z.cols), F32),
            pltpu.VMEM((z.groups, pair, z.cols), BF16),
            pltpu.VMEM((z.groups, z.cap, pair), F32),
            pltpu.VMEM((hg, z.cap, pair), F32),
            pltpu.VMEM((z.nx, z.cap, pair), F32),
            pltpu.VMEM((z.ny, z.cap, pair), F32),
            pltpu.VMEM((2, z.cap, pair), F32),
            pltpu.VMEM((z.ny, quarter, pair), F32),
            pltpu.VMEM((z.nx, quarter, pair), F32),
            pltpu.VMEM((z.nz, 8, pair), F32),
            pltpu.VMEM((z.nz, 8, pair), F32),
            pltpu.VMEM((z.groups, z.blocks, 16, z.cap), BF16),
            pltpu.VMEM((z.nz, 8, 128), F32),
            pltpu.VMEM((z.ny, 8, 128), F32),
            pltpu.VMEM((z.nx, 8, 128), F32),
            pltpu.VMEM((z.nx, 8, 128), F32),
            pltpu.VMEM((z.ny, 8, 128), F32),
            pltpu.VMEM((2, 2, 8, 128), F32),
            pltpu.VMEM((slots, 2 * z.cols), BF16),
            pltpu.VMEM((z.ny, z.rows, z.cols), F32),
            pltpu.SemaphoreType.DMA((count,)),
        ],
        compiler_params=pltpu.CompilerParams(
            collective_id=1, has_side_effects=True, vmem_limit_bytes=56 * 1024 * 1024),
        name="grouped",
    )(student, teacher, group_ids.reshape(1, z.samples), group_ids.reshape(z.samples, 1), bw_table, bw_index)
    return force, loss[0, 0]


def dense_path(z, student, teacher, bw_table, bw_index, group_ids):
    students = lax.all_gather(student, "pair", axis=0, tiled=True)
    teachers = lax.all_gather(teacher, "pair", axis=0, tiled=True)
    both = jnp.concatenate([students, teachers], axis=0)
    wide = both.astype(F32)
    row_wide = student.astype(F32)
    norms = jnp.sum(wide * wide, axis=1)
    row_norms = jnp.sum(row_wide * row_wide, axis=1)
    gram = lax.dot_general(student, both, (((1,), (1,)), ((), ())), preferred_element_type=F32)
    dist = jnp.maximum(lax.psum(row_norms[:, None] + norms[None, :] - 2.0 * gram, "value"), 0.0)
    row_ids = lax.dynamic_slice_in_dim(group_ids, lax.axis_index("pair") * z.rows, z.rows)
    same = (row_ids[:, None] == group_ids[None, :]).astype(F32)
    sizes = jnp.sum(same, axis=1, keepdims=True)
    heights = bw_table[bw_index]
    weight_self, weight_cross, row_loss, pull = pair_terms(
        dist[:, :z.samples], dist[:, z.samples:], same, [heights[m] for m in range(4)], z.latent)
    loss = lax.psum(jnp.sum(row_loss / sizes), "pair") / z.samples
    pulled = row_wide * pull
    pulled = pulled + jnp.dot(weight_self, students, preferred_element_type=F32)
    pulled = pulled - jnp.dot(weight_cross, teachers, preferred_element_type=F32)
    return pulled / sizes, loss


def build(mesh, z):
    def step(student, teacher, bw_table, bw_index, group_ids):
        each = jnp.arange(z.groups, dtype=group_ids.dtype)
        largest = jnp.max(jnp.sum((group_ids[None, :] == each[:, None]).astype(jnp.int32), axis=1))
        return lax.cond(
            largest <= z.cap,
            functools.partial(sorted_path, z),
            functools.partial(dense_path, z),
            student, teacher, bw_table, bw_index, group_ids)

    return jax.shard_map(
        step, mesh=mesh,
        in_specs=(P("pair", "value"), P("pair", "value"), P(None), P(None), P(None)),
        out_specs=(P("pair", "value"), P()),
        check_vma=False)


def solution(mesh):
    return build(mesh, Sizes(ny=4, nx=4, nz=8, nc=2, samples=1536, tile=1024, latent=65536))
```

time: 338 us -> 122 us (0.36)
  blocking collectives: 151 us -> 0 us
  waiting for transfers between devices: 135 us -> 0 us
  Pallas kernels: 0 us -> 97.7 us
  matrix products: 15.8 us -> 0 us
  other arithmetic: 11.7 us -> 1.46 us
    reduce_sum x4 -> x0, blocking collectives: 151 us -> none  [the longest x2 133 us: reference(): norm_student = jnp.sum(student_wide * student_wide, axis=1)]
    pallas_call x0 -> x1, Pallas kernels: none -> 97.7 us  [sorted_path(): pl.pallas_call(functools.partial(fused, z, ids), out_shape=(jax.ShapeDtyp...]
    dot_general x2 -> x0, waiting for transfers between devices: 86.6 us -> none  [reference(): gram_self = jnp.dot(student, student.T, preferred_element_type=jnp.float32)]
    unnamed x4 -> x0, waiting for transfers between devices: 48.5 us -> none
    dot_general x4 -> x0, matrix products: 15.8 us -> none  [the longest x1 4.93 us: reference(): gram_cross = jnp.dot(student, teacher.T, preferred_element_type=jnp.float32)]
    reduce_sum x6 -> x1, other arithmetic: 11.7 us -> 0.82 us  [step(): jnp.sum((group_ids[None, :] == each[:, None]).astype(jnp.int32), axis=1)]
  transfers between devices with their start and end apart: 3 -> 0, of which waited for: 3 -> 0; matrix products, arithmetic and copies ran while one was open for 2% -> 0% of each run, Pallas kernels for 0% -> 0%
where the time goes in v1:
time: 122 us; the launch traced here: 121 us
  Pallas kernels  97.7 us (80%)
  between operations  15.8 us (13%)
  local copies, waits for them, and re-layouts  5.47 us (4%)
  other arithmetic  1.46 us (1%)
    pallas_call x1, Pallas kernels, sorted_path(): pl.pallas_call(functools.partial(fused, z, ids), out_shape=(jax.ShapeDtyp...  97.7 us

profile of v1, /device:TPU:1, one launch (start us, length us, event | category | flops | bytes accessed | tf_op | source)
XLA Modules:
  0.0 121.2 jit_solution(8385535013443574042)
XLA Ops:
  7.2 0.8 convert_reduce_fusion
  8.0 0.6 reduce_max.9
  9.3 102.8 %conditional.1 = (f32[384,1024]{1,0:T(8,128)S(1)}, f32[]{:T(128)}) conditional(s32[]{:T(128)} %convert_element_type.22, (bf16[384,1024]{1,0:T(8,128)(2,1)}, s32[1536]{0:T(1024)}, bf16[384,1024]{1,0:T(8,128)(2,1)}, s32[4]{0:T(128)}, f32[8]{0:T(128)}) %tuple.15, (s32[1536]{0:T(1024)}, bf16[384,1024]{1,0:T(8,128)(2,1)}, bf16[384,1024]{1,0:T(8,128)(2,1)}, ...), branch_computations={%region_2.0_spmd, %region_12.0_spmd} | conditional | flops 4878627840 | bytes 155011872 | solution.py:537
  9.5 1.8 %reshape.34.gc_ref = s32[1536,1]{1,0:T(8,128)} reshape(s32[1536]{0:T(1024)} %get-tuple-element.27) | data formatting | bytes 12288 | tf_op jit(solution)/shard_map/cond/branch_1_fun/reshape | solution.py:506
  11.3 1.3 %reshape.23.gr_ref = s32[1,1536]{1,0:T(1,128)} reshape(s32[1536]{0:T(1024)} %get-tuple-element.27) | data formatting | bytes 12288 | tf_op jit(solution)/shard_map/cond/branch_1_fun/reshape | solution.py:506
  12.6 97.7 %grouped.1 = (f32[384,1024]{1,0:T(8,128)S(1)}, f32[8,128]{1,0:T(8,128)}) custom-call(bf16[384,1024]{1,0:T(8,128)(2,1)} %get-tuple-element.25.s_ref, bf16[384,1024]{1,0:T(8,128)(2,1)} %get-tuple-element.26.t_ref, s32[1,1536]{1,0:T(1,128)} %reshape.23.gr_ref, s32[1536,1]{1,0:T(8,128)} %reshape.34.gc_ref, f32[8]{0:T(128)} %get-tuple-element.28.tab_ref, ...), custom_call_target="tpu_custom_call" | custom-call | tf_op jit(solution)/shard_map/cond/branch_1_fun/grouped/pallas_call | solution.py:471
  110.3 1.2 slice.20
  112.1 1.1 copy.20

commit v2 on v1

--- a/solution.py
+++ b/solution.py
@@ -21,6 +21,7 @@
         self.half = nz // 2
         self.cap = 8 * ny * self.half
         self.blocks = self.cap // 8
+        self.most = self.cap - 3
 
 
 def pair_terms(dist_self, dist_cross, mask, heights, latent):
@@ -63,15 +64,14 @@
     pool = Pool()
     sizes = {
         "in_s": z.ny, "in_t": z.ny, "core": z.groups // 2, "a1": z.nx, "b1": z.ny, "a2": z.ny, "b2": z.nx, "z3": z.nz,
-        "gz_w": z.nz, "gz_t": z.nz, "g2a_w": z.ny, "g2a_t": z.ny, "g2b_w": z.nx, "g2b_t": z.nx,
-        "g1a_w": z.nx, "g1a_t": z.nx, "g1b_w": z.ny, "g1b_t": z.ny, "gc_w": 1, "gc_t": 1, "out": z.ny, "own": 3,
+        "gz": z.nz, "g2a": z.ny, "g2b": z.nx, "g1a": z.nx, "g1b": z.ny, "gc": 1, "out": z.ny, "own": 3,
     }
     return {name: pool.pair(count) for name, count in sizes.items()}, pool.total
 
 
-def fused(z, ids, s_ref, t_ref, gr_ref, gc_ref, tab_ref, idx_ref, f_ref, l_ref,
+def fused(z, ids, s_ref, t_ref, g_ref, tab_ref, idx_ref, f_ref, l_ref,
           xin_s, xin_t, sort_ref, back_ref, xacc, xs, d_ref, rc, r1a, r1b, sums, r2a, r2b, u_ref, r3,
-          wf, t3, t2a, t2b, t1a, t1b, tall, fs, fo, sems):
+          wf, gr_ref, gc_ref, losses, fs, fo, sems):
     y, v = lax.axis_index("pair"), lax.axis_index("value")
     c = lax.rem(v, z.nc)
     x = lax.rem(v // z.nc, z.nx)
@@ -109,6 +109,12 @@
             src_ref=src, dst_ref=dst, send_sem=sems.at[first_send + send], recv_sem=sems.at[first_recv + recv],
             device_id=device, device_id_type=MESH)
 
+    pending = []
+
+    def drain():
+        for one in pending:
+            one.wait_send()
+
     far_first = sorted(range(1, z.ny), key=lambda k: -min(k, z.ny - k))
 
     def in_copy(name, ref, land, k, source, target):
@@ -118,11 +124,23 @@
     for k in far_first:
         in_copy("in_s", s_ref, xin_s, k, y, on_y(k)).start()
         in_copy("in_t", t_ref, xin_t, k, y, on_y(k)).start()
+        pending += [in_copy("in_s", s_ref, xin_s, k, y, on_y(k)), in_copy("in_t", t_ref, xin_t, k, y, on_y(k))]
     own_cols = pl.ds(pl.multiple_of(y * z.cols, z.cols), z.cols)
     own_s = pltpu.make_async_copy(s_ref.at[:, own_cols], xin_s.at[y], sems.at[ids["own"][0]])
     own_t = pltpu.make_async_copy(t_ref.at[:, own_cols], xin_t.at[y], sems.at[ids["own"][0] + 1])
     own_s.start()
     own_t.start()
+
+    gr_ref[...] = g_ref[...].reshape(1, z.samples)
+    corner = (lax.broadcasted_iota(jnp.int32, (z.cap, z.cap), 0) == lax.broadcasted_iota(jnp.int32, (z.cap, z.cap), 1))
+
+    def turn(step, _):
+        first = pl.multiple_of(step * z.cap, z.cap)
+        spread = jnp.where(corner, gr_ref[:, pl.ds(first, z.cap)], 0).astype(F32)
+        gc_ref[pl.ds(first, z.cap), :] = jnp.sum(spread, axis=1, keepdims=True).astype(jnp.int32)
+        return 0
+
+    lax.fori_loop(0, z.samples // z.cap, turn, 0)
 
     chunk = z.rows
     for part in range(z.ny):
@@ -222,6 +240,10 @@
 
     lax.fori_loop(1, z.nx + 1, mine, 0)
 
+    for i in range(hg):
+        pending.append(core_copy(i, other * hg + i))
+    for k in range(1, z.nx):
+        pending += [a1_copy(k, x), b1_copy(k, y)]
     total_a = d_ref[c * hg + x]
     for k in range(1, z.nx):
         source = on_x(z.nx - k)
@@ -235,6 +257,7 @@
 
     for k in range(1, z.ny):
         a2_copy(k, y).start()
+        pending.append(a2_copy(k, y))
     total_b = d_ref[c * hg + z.nx + y]
     for k in range(1, z.ny):
         source = on_y(z.ny - k)
@@ -248,6 +271,7 @@
 
     for k in range(1, z.nx):
         b2_copy(k, x).start()
+        pending.append(b2_copy(k, x))
 
     part_a = sums[0, pl.ds(pl.multiple_of(y * quarter, quarter), quarter), :]
     for k in range(1, z.ny):
@@ -267,6 +291,7 @@
 
     for k in range(1, z.nz):
         z3_copy(k, zc).start()
+        pending.append(z3_copy(k, zc))
 
     def fill_back(step, _):
         first = pl.multiple_of(step * z.cap, z.cap)
@@ -301,91 +326,81 @@
     heights = [tab_ref[idx_ref[m]] for m in range(4)]
     weight_self, weight_cross, row_loss, pull = pair_terms(
         dist[:, 0:z.cap], dist[:, z.cap:2 * z.cap], mask, heights, z.latent)
-    wf[group, block] = jnp.concatenate([weight_self.astype(F32), -weight_cross.astype(F32)], axis=0).astype(BF16)
-    lane = 2 * (member * z.blocks + block)
-    lanes = lax.broadcasted_iota(jnp.int32, (8, 128), 1)
-    t3[zc] = jnp.where(lanes == lane, pull, 0.0) + jnp.where(lanes == lane + 1, row_loss / size, 0.0)
-
-    def gz_copies(k, source):
+    lanes = lax.broadcasted_iota(jnp.int32, (8, z.cap), 1)
+
+    def with_row_term(weights, term):
+        first = term.astype(BF16).astype(F32)
+        second = (term - first).astype(BF16).astype(F32)
+        third = term - first - second
+        columns = jnp.where(lanes == z.cap - 3, first, jnp.where(lanes == z.cap - 2, second, third))
+        return jnp.where(lanes < z.most, weights, columns)
+
+    wf[group, block] = jnp.concatenate(
+        [with_row_term(weight_self.astype(F32), pull), with_row_term(-weight_cross.astype(F32), row_loss / size)],
+        axis=0).astype(BF16)
+
+    def gz_copy(k, source):
         way_of = source // z.half
         group_of = c * hg + way_of * z.nx + (1 - way_of) * x + way_of * y
         block_of = ((1 - way_of) * y + way_of * x) * z.half + lax.rem(source, z.half)
         place = wf.at[group_of, block_of]
-        return (copy("gz_w", place, place, k, source, at(zz=on_z(k))),
-                copy("gz_t", t3.at[source], t3.at[source], k, source, at(zz=on_z(k))))
-
-    def start(pair):
-        for one in pair:
-            one.start()
-
-    def wait_recv(pair):
-        for one in pair:
-            one.wait_recv()
+        return copy("gz", place, place, k, source, at(zz=on_z(k)))
+
+    def start(one):
+        one.start()
+        pending.append(one)
 
     for k in range(1, z.nz):
-        start(gz_copies(k, zc))
+        start(gz_copy(k, zc))
     for k in range(1, z.nz):
-        wait_recv(gz_copies(k, on_z(z.nz - k)))
-    t2a[y] = jnp.sum(t3[0:z.half], axis=0)
-    t2b[x] = jnp.sum(t3[z.half:2 * z.half], axis=0)
-
-    def g2a_copies(k, source):
+        gz_copy(k, on_z(z.nz - k)).wait_recv()
+
+    def g2a_copy(k, source):
         place = wf.at[c * hg + x, pl.ds(source * z.half, z.half)]
-        return (copy("g2a_w", place, place, k, source, at(yy=on_y(k))),
-                copy("g2a_t", t2a.at[source], t2a.at[source], k, source, at(yy=on_y(k))))
-
-    def g2b_copies(k, source):
+        return copy("g2a", place, place, k, source, at(yy=on_y(k)))
+
+    def g2b_copy(k, source):
         place = wf.at[c * hg + z.nx + y, pl.ds(source * z.half, z.half)]
-        return (copy("g2b_w", place, place, k, source, at(xx=on_x(k))),
-                copy("g2b_t", t2b.at[source], t2b.at[source], k, source, at(xx=on_x(k))))
-
-    for k in range(1, z.nx):
-        start(g2a_copies(k, y))
-        start(g2b_copies(k, x))
-
-    def g1a_copies(k, source):
+        return copy("g2b", place, place, k, source, at(xx=on_x(k)))
+
+    for k in range(1, z.nx):
+        start(g2a_copy(k, y))
+        start(g2b_copy(k, x))
+
+    def g1a_copy(k, source):
         place = wf.at[c * hg + source]
-        return (copy("g1a_w", place, place, k, source, at(xx=on_x(k))),
-                copy("g1a_t", t1a.at[source], t1a.at[source], k, source, at(xx=on_x(k))))
-
-    def g1b_copies(k, source):
+        return copy("g1a", place, place, k, source, at(xx=on_x(k)))
+
+    def g1b_copy(k, source):
         place = wf.at[c * hg + z.nx + source]
-        return (copy("g1b_w", place, place, k, source, at(yy=on_y(k))),
-                copy("g1b_t", t1b.at[source], t1b.at[source], k, source, at(yy=on_y(k))))
-
-    for k in range(1, z.ny):
-        wait_recv(g2a_copies(k, on_y(z.ny - k)))
-    t1a[x] = jnp.sum(t2a[...], axis=0)
-    for k in range(1, z.nx):
-        start(g1a_copies(k, x))
-    for k in range(1, z.nx):
-        wait_recv(g2b_copies(k, on_x(z.nx - k)))
-    t1b[y] = jnp.sum(t2b[...], axis=0)
-    for k in range(1, z.ny):
-        start(g1b_copies(k, y))
-    for k in range(1, z.nx):
-        wait_recv(g1a_copies(k, on_x(z.nx - k)))
-    for k in range(1, z.ny):
-        wait_recv(g1b_copies(k, on_y(z.ny - k)))
-    tall[c, 0] = jnp.sum(t1a[...], axis=0)
-    tall[c, 1] = jnp.sum(t1b[...], axis=0)
-
-    def gc_copies(core):
+        return copy("g1b", place, place, k, source, at(yy=on_y(k)))
+
+    for k in range(1, z.ny):
+        g2a_copy(k, on_y(z.ny - k)).wait_recv()
+    for k in range(1, z.nx):
+        start(g1a_copy(k, x))
+    for k in range(1, z.nx):
+        g2b_copy(k, on_x(z.nx - k)).wait_recv()
+    for k in range(1, z.ny):
+        start(g1b_copy(k, y))
+    for k in range(1, z.nx):
+        g1a_copy(k, on_x(z.nx - k)).wait_recv()
+    for k in range(1, z.ny):
+        g1b_copy(k, on_y(z.ny - k)).wait_recv()
+
+    def gc_copy(core):
         place = wf.at[pl.ds(core * hg, hg)]
-        return (copy("gc_w", place, place, 0, 0, at(cc=other)),
-                copy("gc_t", tall.at[core], tall.at[core], 0, 0, at(cc=other)))
-
-    start(gc_copies(c))
+        return copy("gc", place, place, 0, 0, at(cc=other))
+
+    start(gc_copy(c))
 
     def force_of(g):
-        tile = tall[g // hg, lax.rem(g, hg) // z.nx]
-        spot = lax.broadcasted_iota(jnp.int32, (z.blocks, 8, 128), 2)
-        want = 2 * (lax.rem(g, z.nx) * z.blocks + lax.broadcasted_iota(jnp.int32, (z.blocks, 8, 128), 0))
-        picked = jnp.where(spot == want, jnp.broadcast_to(tile[None], (z.blocks, 8, 128)), 0.0)
-        pulls = jnp.sum(picked, axis=2, keepdims=True).reshape(z.cap, 1)
         held = wf[g].astype(F32).reshape(z.blocks, 2, 8, z.cap)
-        weights = jnp.concatenate(
-            [held[:, 0].reshape(z.cap, z.cap), held[:, 1].reshape(z.cap, z.cap)], axis=1).astype(BF16)
+        to_self, to_cross = held[:, 0].reshape(z.cap, z.cap), held[:, 1].reshape(z.cap, z.cap)
+        last = lax.broadcasted_iota(jnp.int32, (z.cap, z.cap), 1) >= z.most
+        pulls = jnp.sum(jnp.where(last, to_self, 0.0), axis=1, keepdims=True)
+        losses[g] = jnp.sum(jnp.where(last, to_cross, 0.0), axis=0, keepdims=True)
+        weights = jnp.concatenate([to_self, to_cross], axis=1).astype(BF16)
         values = xs[g]
         pulled = values[0:z.cap].astype(F32) * pulls + jnp.dot(weights, values, preferred_element_type=F32)
         size_of = jnp.sum(jnp.where(gr_ref[...] == g, 1.0, 0.0), axis=1, keepdims=True)
@@ -405,13 +420,10 @@
         return 0
 
     lax.fori_loop(0, hg, own_force, 0)
-    wait_recv(gc_copies(other))
+    gc_copy(other).wait_recv()
     lax.fori_loop(0, hg, other_force, 0)
 
-    odd = lax.rem(lax.broadcasted_iota(jnp.int32, (8, 128), 1), 2) == 1
-    every = jnp.where(odd, tall[0, 0] + tall[0, 1] + tall[1, 0] + tall[1, 1], 0.0)
-    every = jnp.sum(jnp.sum(every, axis=1, keepdims=True), axis=0, keepdims=True)
-    l_ref[...] = jnp.broadcast_to(every / z.samples, l_ref.shape)
+    l_ref[...] = jnp.sum(jnp.sum(losses[...], axis=0), axis=1, keepdims=True) / z.samples
 
     def out_copy(k, source):
         cols = pl.ds(pl.multiple_of(source * z.cols, z.cols), z.cols)
@@ -441,26 +453,8 @@
         out_copy(k, on_y(z.ny - k)).wait_recv()
 
     for k in range(1, z.ny):
-        in_copy("in_s", s_ref, xin_s, k, y, on_y(k)).wait_send()
-        in_copy("in_t", t_ref, xin_t, k, y, on_y(k)).wait_send()
-        b1_copy(k, y).wait_send()
-        a2_copy(k, y).wait_send()
-        out_copy(k, y).wait_send()
-        for one in g2a_copies(k, y) + g1b_copies(k, y):
-            one.wait_send()
-    for k in range(1, z.nx):
-        a1_copy(k, x).wait_send()
-        b2_copy(k, x).wait_send()
-        for one in g2b_copies(k, x) + g1a_copies(k, x):
-            one.wait_send()
-    for k in range(1, z.nz):
-        z3_copy(k, zc).wait_send()
-        for one in gz_copies(k, zc):
-            one.wait_send()
-    for i in range(hg):
-        core_copy(i, other * hg + i).wait_send()
-    for one in gc_copies(c):
-        one.wait_send()
+        pending.append(out_copy(k, y))
+    drain()
 
 
 def sorted_path(z, student, teacher, bw_table, bw_index, group_ids):
@@ -470,8 +464,8 @@
     vmem, smem, anywhere = (pl.BlockSpec(memory_space=m) for m in (pltpu.VMEM, pltpu.SMEM, pl.ANY))
     force, loss = pl.pallas_call(
         functools.partial(fused, z, ids),
-        out_shape=(jax.ShapeDtypeStruct((z.rows, z.tile), F32), jax.ShapeDtypeStruct((8, 128), F32)),
-        in_specs=[anywhere, anywhere, vmem, vmem, smem, smem],
+        out_shape=(jax.ShapeDtypeStruct((z.rows, z.tile), F32), jax.ShapeDtypeStruct((1, 1), F32)),
+        in_specs=[anywhere, anywhere, vmem, smem, smem],
         out_specs=(anywhere, vmem),
         scratch_shapes=[
             pltpu.VMEM((z.ny, z.rows, z.cols), BF16),
@@ -490,12 +484,9 @@
             pltpu.VMEM((z.nz, 8, pair), F32),
             pltpu.VMEM((z.nz, 8, pair), F32),
             pltpu.VMEM((z.groups, z.blocks, 16, z.cap), BF16),
-            pltpu.VMEM((z.nz, 8, 128), F32),
-            pltpu.VMEM((z.ny, 8, 128), F32),
-            pltpu.VMEM((z.nx, 8, 128), F32),
-            pltpu.VMEM((z.nx, 8, 128), F32),
-            pltpu.VMEM((z.ny, 8, 128), F32),
-            pltpu.VMEM((2, 2, 8, 128), F32),
+            pltpu.VMEM((1, z.samples), jnp.int32),
+            pltpu.VMEM((z.samples, 1), jnp.int32),
+            pltpu.VMEM((z.groups, 1, z.cap), F32),
             pltpu.VMEM((slots, 2 * z.cols), BF16),
             pltpu.VMEM((z.ny, z.rows, z.cols), F32),
             pltpu.SemaphoreType.DMA((count,)),
@@ -503,27 +494,45 @@
         compiler_params=pltpu.CompilerParams(
             collective_id=1, has_side_effects=True, vmem_limit_bytes=56 * 1024 * 1024),
         name="grouped",
-    )(student, teacher, group_ids.reshape(1, z.samples), group_ids.reshape(z.samples, 1), bw_table, bw_index)
-    return force, loss[0, 0]
+    )(student, teacher, group_ids, bw_table, bw_index)
+    return force, loss.reshape(())
+
+
+def gather_pair(z, block):
+    y = lax.axis_index("pair")
+    out = jnp.zeros((z.ny,) + block.shape, block.dtype)
+    for k in range(z.ny):
+        moved = lax.ppermute(block, "pair", [(i, (i + k) % z.ny) for i in range(z.ny)]) if k else block
+        out = lax.dynamic_update_index_in_dim(out, moved, lax.rem(y + z.ny - k, z.ny), 0)
+    return out.reshape((z.ny * block.shape[0],) + block.shape[1:])
+
+
+def sum_over(array, axis, count):
+    step = 1
+    while step < count:
+        array = array + lax.ppermute(array, axis, [(i, i ^ step) for i in range(count)])
+        step *= 2
+    return array
 
 
 def dense_path(z, student, teacher, bw_table, bw_index, group_ids):
-    students = lax.all_gather(student, "pair", axis=0, tiled=True)
-    teachers = lax.all_gather(teacher, "pair", axis=0, tiled=True)
+    students = gather_pair(z, student)
+    teachers = gather_pair(z, teacher)
     both = jnp.concatenate([students, teachers], axis=0)
     wide = both.astype(F32)
     row_wide = student.astype(F32)
     norms = jnp.sum(wide * wide, axis=1)
     row_norms = jnp.sum(row_wide * row_wide, axis=1)
     gram = lax.dot_general(student, both, (((1,), (1,)), ((), ())), preferred_element_type=F32)
-    dist = jnp.maximum(lax.psum(row_norms[:, None] + norms[None, :] - 2.0 * gram, "value"), 0.0)
+    part = row_norms[:, None] + norms[None, :] - 2.0 * gram
+    dist = jnp.maximum(sum_over(part, "value", z.nx * z.nz * z.nc), 0.0)
     row_ids = lax.dynamic_slice_in_dim(group_ids, lax.axis_index("pair") * z.rows, z.rows)
     same = (row_ids[:, None] == group_ids[None, :]).astype(F32)
     sizes = jnp.sum(same, axis=1, keepdims=True)
     heights = bw_table[bw_index]
     weight_self, weight_cross, row_loss, pull = pair_terms(
         dist[:, :z.samples], dist[:, z.samples:], same, [heights[m] for m in range(4)], z.latent)
-    loss = lax.psum(jnp.sum(row_loss / sizes), "pair") / z.samples
+    loss = sum_over(jnp.broadcast_to(jnp.sum(row_loss / sizes), (8, 128)), "pair", z.ny)[0, 0] / z.samples
     pulled = row_wide * pull
     pulled = pulled + jnp.dot(weight_self, students, preferred_element_type=F32)
     pulled = pulled - jnp.dot(weight_cross, teachers, preferred_element_type=F32)
@@ -535,7 +544,7 @@
         each = jnp.arange(z.groups, dtype=group_ids.dtype)
         largest = jnp.max(jnp.sum((group_ids[None, :] == each[:, None]).astype(jnp.int32), axis=1))
         return lax.cond(
-            largest <= z.cap,
+            largest <= z.most,
             functools.partial(sorted_path, z),
             functools.partial(dense_path, z),
             student, teacher, bw_table, bw_index, group_ids)

time: 122 us -> 103 us (0.84)
  between operations: 15.8 us -> 2.42 us
  local copies, waits for them, and re-layouts: 5.47 us -> 1.15 us
    reshape x2 -> x0, local copies, waits for them, and re-layouts: 3.14 us -> none  [the longest x1 1.85 us: sorted_path(): group_ids.reshape(z.samples, 1)]
where the time goes in v2:
time: 103 us; the launch traced here: 102 us
  Pallas kernels  96.5 us (94%)
  between operations  2.42 us (2%)
  other arithmetic  1.46 us (1%)
  local copies, waits for them, and re-layouts  1.15 us (1%)
    pallas_call x1, Pallas kernels, sorted_path(): pl.pallas_call(functools.partial(fused, z, ids), out_shape=(jax.ShapeDtyp...  96.5 us

profile of v2, /device:TPU:1, one launch (start us, length us, event | category | flops | bytes accessed | tf_op | source)
XLA Modules:
  0.0 102.4 jit_solution(4627439733795942891)
XLA Ops:
  0.6 0.8 convert_reduce_fusion
  1.5 0.6 reduce_max.9
  2.7 97.3 %conditional.1 = (f32[384,1024]{1,0:T(8,128)S(1)}, f32[]{:T(128)}) conditional(s32[]{:T(128)} %convert_element_type.22, (bf16[384,1024]{1,0:T(8,128)(2,1)}, s32[1536]{0:T(1024)}, bf16[384,1024]{1,0:T(8,128)(2,1)}, s32[4]{0:T(128)}, f32[8]{0:T(128)}) %tuple.15, (bf16[384,1024]{1,0:T(8,128)(2,1)}, bf16[384,1024]{1,0:T(8,128)(2,1)}, s32[1536]{0:T(1024)}, ...), branch_computations={%region_2.10_spmd, %region_10.11_spmd} | conditional | flops 4906549248 | bytes 310783680 | solution.py:546
  3.0 96.5 %grouped.1 = (f32[384,1024]{1,0:T(8,128)S(1)}, f32[1,1]{1,0:T(1,128)}) custom-call(bf16[384,1024]{1,0:T(8,128)(2,1)} %get-tuple-element.25.s_ref, bf16[384,1024]{1,0:T(8,128)(2,1)} %get-tuple-element.26.t_ref, s32[1536]{0:T(1024)} %get-tuple-element.27.g_ref, f32[8]{0:T(128)} %get-tuple-element.28.tab_ref, s32[4]{0:T(128)} %get-tuple-element.29.idx_ref), custom_call_target="tpu_custom_call" | custom-call | tf_op jit(solution)/shard_map/cond/branch_1_fun/grouped/pallas_call | solution.py:465
  100.1 1.1 %copy.25 = f32[384,1024]{1,0:T(8,128)} copy(f32[384,1024]{1,0:T(8,128)S(1)} %get-tuple-element.62) | data formatting | bytes 3145728

commit v3 on v2

--- a/solution.py
+++ b/solution.py
@@ -9,6 +9,9 @@
 
 MESH = pl.DeviceIdType.MESH
 F32, BF16 = jnp.float32, jnp.bfloat16
+
+
+TOGETHER = 4
 
 
 class Sizes:
@@ -22,6 +25,7 @@
         self.cap = 8 * ny * self.half
         self.blocks = self.cap // 8
         self.most = self.cap - 3
+        self.lanes = min(128, self.rows)
 
 
 def pair_terms(dist_self, dist_cross, mask, heights, latent):
@@ -64,14 +68,14 @@
     pool = Pool()
     sizes = {
         "in_s": z.ny, "in_t": z.ny, "core": z.groups // 2, "a1": z.nx, "b1": z.ny, "a2": z.ny, "b2": z.nx, "z3": z.nz,
-        "gz": z.nz, "g2a": z.ny, "g2b": z.nx, "g1a": z.nx, "g1b": z.ny, "gc": 1, "out": z.ny, "own": 3,
+        "gz": z.nz, "g2a": z.ny, "g2b": z.nx, "g1a": z.nx, "g1b": z.ny, "gc": 1, "out": z.ny, "scale": z.ny, "own": 3,
     }
     return {name: pool.pair(count) for name, count in sizes.items()}, pool.total
 
 
-def fused(z, ids, s_ref, t_ref, g_ref, tab_ref, idx_ref, f_ref, l_ref,
+def fused(z, ids, s_ref, t_ref, g_ref, tab_ref, idx_ref, q_ref, scale_ref, l_ref, most_ref,
           xin_s, xin_t, sort_ref, back_ref, xacc, xs, d_ref, rc, r1a, r1b, sums, r2a, r2b, u_ref, r3,
-          wf, gr_ref, gc_ref, losses, fs, fo, sems):
+          wf, gr_ref, gc_ref, losses, fs, qs, scales, landed, sems):
     y, v = lax.axis_index("pair"), lax.axis_index("value")
     c = lax.rem(v, z.nc)
     x = lax.rem(v // z.nc, z.nx)
@@ -115,13 +119,13 @@
         for one in pending:
             one.wait_send()
 
-    far_first = sorted(range(1, z.ny), key=lambda k: -min(k, z.ny - k))
+    order = sorted(range(1, z.ny), key=lambda k: min(k, z.ny - k))
 
     def in_copy(name, ref, land, k, source, target):
         cols = pl.ds(pl.multiple_of(target * z.cols, z.cols), z.cols)
         return copy(name, ref.at[:, cols], land.at[source], k, source, at(yy=on_y(k)))
 
-    for k in far_first:
+    for k in order:
         in_copy("in_s", s_ref, xin_s, k, y, on_y(k)).start()
         in_copy("in_t", t_ref, xin_t, k, y, on_y(k)).start()
         pending += [in_copy("in_s", s_ref, xin_s, k, y, on_y(k)), in_copy("in_t", t_ref, xin_t, k, y, on_y(k))]
@@ -143,6 +147,7 @@
     lax.fori_loop(0, z.samples // z.cap, turn, 0)
 
     chunk = z.rows
+    largest = jnp.zeros((1, 1), jnp.int32)
     for part in range(z.ny):
         cols = pl.ds(part * chunk, chunk)
         ids_row = gr_ref[:, cols]
@@ -156,6 +161,7 @@
             return rank + jnp.sum(hit, axis=0, keepdims=True)
 
         rank = lax.fori_loop(0, z.samples // z.cap, count_before, jnp.zeros((1, chunk), jnp.int32))
+        largest = jnp.maximum(largest, jnp.max(rank, axis=1, keepdims=True) + 1)
         place = ids_row * z.cap + rank
 
         def fill_sort(step, _):
@@ -166,132 +172,8 @@
 
         lax.fori_loop(0, z.groups, fill_sort, 0)
 
-    own_s.wait()
-    own_t.wait()
-
-    xacc[...] = jnp.zeros_like(xacc)
+    most_ref[...] = largest
     slots = z.groups * z.cap
-    tall_rows = slots // 4
-
-    def sort_from(source):
-        def body(step, _):
-            first = pl.multiple_of(step * tall_rows, tall_rows)
-            place = sort_ref[source, pl.ds(first, tall_rows), :]
-            xacc[pl.ds(first, tall_rows), 0:z.cols] += jnp.dot(place, xin_s[source], preferred_element_type=F32)
-            xacc[pl.ds(first, tall_rows), z.cols:2 * z.cols] += jnp.dot(place, xin_t[source], preferred_element_type=F32)
-            return 0
-
-        lax.fori_loop(0, 4, body, 0)
-
-    sort_from(y)
-    for k in reversed(far_first):
-        source = on_y(z.ny - k)
-        in_copy("in_s", s_ref, xin_s, k, source, on_y(k)).wait_recv()
-        in_copy("in_t", t_ref, xin_t, k, source, on_y(k)).wait_recv()
-        sort_from(source)
-
-    def distances(group):
-        rows = pl.ds(pl.multiple_of(group * z.cap, z.cap), z.cap)
-        both = jnp.concatenate([xacc[rows, 0:z.cols], xacc[rows, z.cols:2 * z.cols]], axis=0).astype(BF16)
-        xs[group] = both
-        gram = lax.dot_general(both, both, (((1,), (1,)), ((), ())), preferred_element_type=F32)
-        size = 2 * z.cap
-        eye = lax.broadcasted_iota(jnp.int32, (size, size), 0) == lax.broadcasted_iota(jnp.int32, (size, size), 1)
-        diagonal = jnp.where(eye, gram, 0.0)
-        norm_row = jnp.sum(diagonal, axis=0, keepdims=True)
-        norm_col = jnp.sum(diagonal[0:z.cap], axis=1, keepdims=True)
-        d_ref[group] = norm_col + norm_row - 2.0 * gram[0:z.cap]
-
-    def core_copy(i, group):
-        return copy("core", d_ref.at[group], rc.at[i], i, i, at(cc=other))
-
-    def to_other(i, _):
-        distances(other * hg + i)
-        core_copy(i, other * hg + i).start()
-        return 0
-
-    lax.fori_loop(0, hg, to_other, 0)
-
-    def a1_copy(k, source):
-        return copy("a1", d_ref.at[c * hg + on_x(k)], r1a.at[source], k, source, at(xx=on_x(k)))
-
-    def b1_copy(k, source):
-        return copy("b1", d_ref.at[c * hg + z.nx + on_y(k)], r1b.at[source], k, source, at(yy=on_y(k)))
-
-    def add_core(i):
-        distances(c * hg + i)
-        core_copy(i, c * hg + i).wait_recv()
-        d_ref[c * hg + i] += rc[i]
-
-    def mine(k, _):
-        add_core(on_x(k))
-
-        @pl.when(k < z.nx)
-        def _():
-            a1_copy(k, x).start()
-
-        add_core(z.nx + on_y(k))
-
-        @pl.when(k < z.nx)
-        def _():
-            b1_copy(k, y).start()
-
-        return 0
-
-    lax.fori_loop(1, z.nx + 1, mine, 0)
-
-    for i in range(hg):
-        pending.append(core_copy(i, other * hg + i))
-    for k in range(1, z.nx):
-        pending += [a1_copy(k, x), b1_copy(k, y)]
-    total_a = d_ref[c * hg + x]
-    for k in range(1, z.nx):
-        source = on_x(z.nx - k)
-        a1_copy(k, source).wait_recv()
-        total_a = total_a + r1a[source]
-    sums[0] = total_a
-
-    def a2_copy(k, source):
-        rows = pl.ds(pl.multiple_of(on_y(k) * quarter, quarter), quarter)
-        return copy("a2", sums.at[0, rows], r2a.at[source], k, source, at(yy=on_y(k)))
-
-    for k in range(1, z.ny):
-        a2_copy(k, y).start()
-        pending.append(a2_copy(k, y))
-    total_b = d_ref[c * hg + z.nx + y]
-    for k in range(1, z.ny):
-        source = on_y(z.ny - k)
-        b1_copy(k, source).wait_recv()
-        total_b = total_b + r1b[source]
-    sums[1] = total_b
-
-    def b2_copy(k, source):
-        rows = pl.ds(pl.multiple_of(on_x(k) * quarter, quarter), quarter)
-        return copy("b2", sums.at[1, rows], r2b.at[source], k, source, at(xx=on_x(k)))
-
-    for k in range(1, z.nx):
-        b2_copy(k, x).start()
-        pending.append(b2_copy(k, x))
-
-    part_a = sums[0, pl.ds(pl.multiple_of(y * quarter, quarter), quarter), :]
-    for k in range(1, z.ny):
-        source = on_y(z.ny - k)
-        a2_copy(k, source).wait_recv()
-        part_a = part_a + r2a[source]
-    u_ref[0:z.half] = part_a.reshape(z.half, 8, 2 * z.cap)
-    part_b = sums[1, pl.ds(pl.multiple_of(x * quarter, quarter), quarter), :]
-    for k in range(1, z.nx):
-        source = on_x(z.nx - k)
-        b2_copy(k, source).wait_recv()
-        part_b = part_b + r2b[source]
-    u_ref[z.half:2 * z.half] = part_b.reshape(z.half, 8, 2 * z.cap)
-
-    def z3_copy(k, source):
-        return copy("z3", u_ref.at[on_z(k)], r3.at[source], k, source, at(zz=on_z(k)))
-
-    for k in range(1, z.nz):
-        z3_copy(k, zc).start()
-        pending.append(z3_copy(k, zc))
 
     def fill_back(step, _):
         first = pl.multiple_of(step * z.cap, z.cap)
@@ -306,6 +188,135 @@
         return 0
 
     lax.fori_loop(0, z.samples // z.cap, fill_back, 0)
+
+    own_s.wait()
+    own_t.wait()
+
+    xacc[...] = jnp.zeros_like(xacc)
+    tall_rows = slots // 4
+
+    def sort_from(source):
+        def body(step, _):
+            first = pl.multiple_of(step * tall_rows, tall_rows)
+            place = sort_ref[source, pl.ds(first, tall_rows), :]
+            xacc[pl.ds(first, tall_rows), 0:z.cols] += jnp.dot(place, xin_s[source], preferred_element_type=F32)
+            xacc[pl.ds(first, tall_rows), z.cols:2 * z.cols] += jnp.dot(place, xin_t[source], preferred_element_type=F32)
+            return 0
+
+        lax.fori_loop(0, 4, body, 0)
+
+    sort_from(y)
+    for k in order:
+        source = on_y(z.ny - k)
+        in_copy("in_s", s_ref, xin_s, k, source, on_y(k)).wait_recv()
+        in_copy("in_t", t_ref, xin_t, k, source, on_y(k)).wait_recv()
+        sort_from(source)
+
+    def distances(groups):
+        size = 2 * z.cap
+        eye = lax.broadcasted_iota(jnp.int32, (size, size), 0) == lax.broadcasted_iota(jnp.int32, (size, size), 1)
+        found = []
+        for group in groups:
+            rows = pl.ds(pl.multiple_of(group * z.cap, z.cap), z.cap)
+            both = jnp.concatenate([xacc[rows, 0:z.cols], xacc[rows, z.cols:2 * z.cols]], axis=0).astype(BF16)
+            gram = lax.dot_general(both, both, (((1,), (1,)), ((), ())), preferred_element_type=F32)
+            found.append((both, gram))
+        parts = []
+        for both, gram in found:
+            diagonal = jnp.where(eye, gram, 0.0)
+            norm_row = jnp.sum(diagonal, axis=0, keepdims=True)
+            norm_col = jnp.sum(diagonal[0:z.cap], axis=1, keepdims=True)
+            parts.append(norm_col + norm_row - 2.0 * gram[0:z.cap])
+        for group, (both, _), part in zip(groups, found, parts):
+            xs[group] = both
+            d_ref[group] = part
+
+    def core_copy(i, group):
+        return copy("core", d_ref.at[group], rc.at[i], i, i, at(cc=other))
+
+    def to_other(i, _):
+        now = [TOGETHER * i + n for n in range(TOGETHER)]
+        distances([other * hg + n for n in now])
+        for n in now:
+            core_copy(n, other * hg + n).start()
+        return 0
+
+    lax.fori_loop(0, hg // TOGETHER, to_other, 0)
+
+    def a1_copy(k, source):
+        return copy("a1", d_ref.at[c * hg + on_x(k)], r1a.at[source], k, source, at(xx=on_x(k)))
+
+    def b1_copy(k, source):
+        return copy("b1", d_ref.at[c * hg + z.nx + on_y(k)], r1b.at[source], k, source, at(yy=on_y(k)))
+
+    def mine(k, _):
+        now = (on_x(k), z.nx + on_y(k))
+        distances([c * hg + i for i in now])
+        for i in now:
+            core_copy(i, c * hg + i).wait_recv()
+            d_ref[c * hg + i] += rc[i]
+
+        @pl.when(k < z.nx)
+        def _():
+            a1_copy(k, x).start()
+            b1_copy(k, y).start()
+
+        return 0
+
+    lax.fori_loop(1, z.nx + 1, mine, 0)
+
+    for i in range(hg):
+        pending.append(core_copy(i, other * hg + i))
+    for k in range(1, z.nx):
+        pending += [a1_copy(k, x), b1_copy(k, y)]
+    total_a = d_ref[c * hg + x]
+    for k in range(1, z.nx):
+        source = on_x(z.nx - k)
+        a1_copy(k, source).wait_recv()
+        total_a = total_a + r1a[source]
+    sums[0] = total_a
+
+    def a2_copy(k, source):
+        rows = pl.ds(pl.multiple_of(on_y(k) * quarter, quarter), quarter)
+        return copy("a2", sums.at[0, rows], r2a.at[source], k, source, at(yy=on_y(k)))
+
+    for k in range(1, z.ny):
+        a2_copy(k, y).start()
+        pending.append(a2_copy(k, y))
+    total_b = d_ref[c * hg + z.nx + y]
+    for k in range(1, z.ny):
+        source = on_y(z.ny - k)
+        b1_copy(k, source).wait_recv()
+        total_b = total_b + r1b[source]
+    sums[1] = total_b
+
+    def b2_copy(k, source):
+        rows = pl.ds(pl.multiple_of(on_x(k) * quarter, quarter), quarter)
+        return copy("b2", sums.at[1, rows], r2b.at[source], k, source, at(xx=on_x(k)))
+
+    for k in range(1, z.nx):
+        b2_copy(k, x).start()
+        pending.append(b2_copy(k, x))
+
+    part_a = sums[0, pl.ds(pl.multiple_of(y * quarter, quarter), quarter), :]
+    for k in range(1, z.ny):
+        source = on_y(z.ny - k)
+        a2_copy(k, source).wait_recv()
+        part_a = part_a + r2a[source]
+    u_ref[0:z.half] = part_a.reshape(z.half, 8, 2 * z.cap)
+    part_b = sums[1, pl.ds(pl.multiple_of(x * quarter, quarter), quarter), :]
+    for k in range(1, z.nx):
+        source = on_x(z.nx - k)
+        b2_copy(k, source).wait_recv()
+        part_b = part_b + r2b[source]
+    u_ref[z.half:2 * z.half] = part_b.reshape(z.half, 8, 2 * z.cap)
+
+    def z3_copy(k, source):
+        return copy("z3", u_ref.at[on_z(k)], r3.at[source], k, source, at(zz=on_z(k)))
+
+    for k in range(1, z.nz):
+        z3_copy(k, zc).start()
+        pending.append(z3_copy(k, zc))
 
     dist = u_ref[zc]
     for k in range(1, z.nz):
@@ -394,66 +405,90 @@
 
     start(gc_copy(c))
 
-    def force_of(g):
-        held = wf[g].astype(F32).reshape(z.blocks, 2, 8, z.cap)
-        to_self, to_cross = held[:, 0].reshape(z.cap, z.cap), held[:, 1].reshape(z.cap, z.cap)
-        last = lax.broadcasted_iota(jnp.int32, (z.cap, z.cap), 1) >= z.most
-        pulls = jnp.sum(jnp.where(last, to_self, 0.0), axis=1, keepdims=True)
-        losses[g] = jnp.sum(jnp.where(last, to_cross, 0.0), axis=0, keepdims=True)
-        weights = jnp.concatenate([to_self, to_cross], axis=1).astype(BF16)
-        values = xs[g]
-        pulled = values[0:z.cap].astype(F32) * pulls + jnp.dot(weights, values, preferred_element_type=F32)
-        size_of = jnp.sum(jnp.where(gr_ref[...] == g, 1.0, 0.0), axis=1, keepdims=True)
-        force = pulled / size_of
-        high = force.astype(BF16)
-        low = (force - high.astype(F32)).astype(BF16)
-        rows = pl.ds(pl.multiple_of(g * z.cap, z.cap), z.cap)
-        fs[rows, 0:z.cols] = high
-        fs[rows, z.cols:2 * z.cols] = low
+    last = lax.broadcasted_iota(jnp.int32, (z.cap, z.cap), 1) >= z.most
+
+    def force_of(groups):
+        found = []
+        for g in groups:
+            held = wf[g].astype(F32).reshape(z.blocks, 2, 8, z.cap)
+            to_self, to_cross = held[:, 0].reshape(z.cap, z.cap), held[:, 1].reshape(z.cap, z.cap)
+            pulls = jnp.sum(jnp.where(last, to_self, 0.0), axis=1, keepdims=True)
+            loss = jnp.sum(jnp.where(last, to_cross, 0.0), axis=0, keepdims=True)
+            weights = jnp.concatenate([to_self, to_cross], axis=1).astype(BF16)
+            values = xs[g]
+            pulled = values[0:z.cap].astype(F32) * pulls + jnp.dot(weights, values, preferred_element_type=F32)
+            size_of = jnp.sum(jnp.where(gr_ref[...] == g, 1.0, 0.0), axis=1, keepdims=True)
+            force = pulled / size_of
+            high = force.astype(BF16)
+            low = (force - high.astype(F32)).astype(BF16)
+            found.append((loss, high, low))
+        for g, (loss, high, low) in zip(groups, found):
+            rows = pl.ds(pl.multiple_of(g * z.cap, z.cap), z.cap)
+            losses[g] = loss
+            fs[rows, 0:z.cols] = high
+            fs[rows, z.cols:2 * z.cols] = low
 
     def own_force(i, _):
-        force_of(c * hg + i)
+        force_of([c * hg + TOGETHER * i + n for n in range(TOGETHER)])
         return 0
 
     def other_force(i, _):
-        force_of(other * hg + i)
+        force_of([other * hg + TOGETHER * i + n for n in range(TOGETHER)])
         return 0
 
-    lax.fori_loop(0, hg, own_force, 0)
+    lax.fori_loop(0, hg // TOGETHER, own_force, 0)
     gc_copy(other).wait_recv()
-    lax.fori_loop(0, hg, other_force, 0)
+    lax.fori_loop(0, hg // TOGETHER, other_force, 0)
 
     l_ref[...] = jnp.sum(jnp.sum(losses[...], axis=0), axis=1, keepdims=True) / z.samples
 
-    def out_copy(k, source):
+    def out_copies(k, source):
         cols = pl.ds(pl.multiple_of(source * z.cols, z.cols), z.cols)
-        return copy("out", fo.at[k], f_ref.at[:, cols], k, source, at(yy=on_y(k)))
-
-    def out_local():
-        return pltpu.make_async_copy(fo.at[0], f_ref.at[:, own_cols], sems.at[ids["own"][0] + 2])
+        return (copy("out", qs.at[k], q_ref.at[:, cols], k, source, at(yy=on_y(k))),
+                copy("scale", scales.at[k], landed.at[source], k, source, at(yy=on_y(k))))
+
+    parts = z.rows // z.lanes
+    square = (z.lanes, z.lanes)
+    same = lax.broadcasted_iota(jnp.int32, square, 0) == lax.broadcasted_iota(jnp.int32, square, 1)
 
     def unsort(k):
         rows = pl.ds(pl.multiple_of(on_y(k) * z.rows, z.rows), z.rows)
         moved = jnp.dot(back_ref[rows, :], fs[...], preferred_element_type=F32)
-        fo[k] = moved[:, 0:z.cols] + moved[:, z.cols:2 * z.cols]
+        force = moved[:, 0:z.cols] + moved[:, z.cols:2 * z.cols]
+        top = jnp.maximum(jnp.max(jnp.abs(force), axis=1, keepdims=True), 1e-33)
+        qs[k] = jnp.round(force * (32767.0 / top)).astype(jnp.int32).astype(jnp.int16)
+        step = top / 32767.0
+        for part in range(parts):
+            spread = jnp.where(same, step[part * z.lanes:(part + 1) * z.lanes], 0.0)
+            scales[k, part:part + 1, :] = jnp.sum(spread, axis=0, keepdims=True)
 
     def send_out(step, _):
-        k = step if z.ny == 2 else lax.rem(step + z.ny // 2 - 1, z.ny - 1) + 1
-        if z.ny == 2:
-            k = 1
+        k = lax.rem(step + z.ny // 2 - 1, z.ny - 1) + 1
         unsort(k)
-        out_copy(k, y).start()
+        for one in out_copies(k, y):
+            one.start()
         return 0
 
+    scales[...] = jnp.zeros_like(scales)
     lax.fori_loop(0, z.ny - 1, send_out, 0)
     unsort(0)
-    out_local().start()
-    out_local().wait()
-    for k in range(1, z.ny):
-        out_copy(k, on_y(z.ny - k)).wait_recv()
-
-    for k in range(1, z.ny):
-        pending.append(out_copy(k, y))
+    local = pltpu.make_async_copy(qs.at[0], q_ref.at[:, own_cols], sems.at[ids["own"][0] + 2])
+    local.start()
+    landed[y] = scales[0]
+    for k in range(1, z.ny):
+        for one in out_copies(k, on_y(z.ny - k)):
+            one.wait_recv()
+    for part in range(parts):
+        at_lane = lax.broadcasted_iota(jnp.int32, (z.lanes, 128), 1)
+        column = jnp.zeros((z.lanes, 128), F32)
+        for source in range(z.ny):
+            spread = jnp.where(same, landed[source, part:part + 1, :], 0.0)
+            column = jnp.where(at_lane == source, jnp.sum(spread, axis=1, keepdims=True), column)
+        scale_ref[part * z.lanes:(part + 1) * z.lanes, :] = column
+    local.wait()
+
+    for k in range(1, z.ny):
+        pending += out_copies(k, y)
     drain()
 
 
@@ -462,11 +497,12 @@
     slots, pair, hg = z.groups * z.cap, 2 * z.cap, z.groups // 2
     quarter = z.cap // z.ny
     vmem, smem, anywhere = (pl.BlockSpec(memory_space=m) for m in (pltpu.VMEM, pltpu.SMEM, pl.ANY))
-    force, loss = pl.pallas_call(
+    sent, scale, loss, largest = pl.pallas_call(
         functools.partial(fused, z, ids),
-        out_shape=(jax.ShapeDtypeStruct((z.rows, z.tile), F32), jax.ShapeDtypeStruct((1, 1), F32)),
+        out_shape=(jax.ShapeDtypeStruct((z.rows, z.tile), jnp.int16), jax.ShapeDtypeStruct((z.rows, 128), F32),
+                   jax.ShapeDtypeStruct((1, 1), F32), jax.ShapeDtypeStruct((1, 1), jnp.int32)),
         in_specs=[anywhere, anywhere, vmem, smem, smem],
-        out_specs=(anywhere, vmem),
+        out_specs=(anywhere, vmem, vmem, vmem),
         scratch_shapes=[
             pltpu.VMEM((z.ny, z.rows, z.cols), BF16),
             pltpu.VMEM((z.ny, z.rows, z.cols), BF16),
@@ -488,14 +524,16 @@
             pltpu.VMEM((z.samples, 1), jnp.int32),
             pltpu.VMEM((z.groups, 1, z.cap), F32),
             pltpu.VMEM((slots, 2 * z.cols), BF16),
-            pltpu.VMEM((z.ny, z.rows, z.cols), F32),
+            pltpu.VMEM((z.ny, z.rows, z.cols), jnp.int16),
+            pltpu.VMEM((z.ny, 8, z.lanes), F32),
+            pltpu.VMEM((z.ny, 8, z.lanes), F32),
             pltpu.SemaphoreType.DMA((count,)),
         ],
         compiler_params=pltpu.CompilerParams(
             collective_id=1, has_side_effects=True, vmem_limit_bytes=56 * 1024 * 1024),
         name="grouped",
     )(student, teacher, group_ids, bw_table, bw_index)
-    return force, loss.reshape(())
+    return sent, scale, loss.reshape(()), largest.reshape(())
 
 
 def gather_pair(z, block):
@@ -539,15 +577,22 @@
     return pulled / sizes, loss
 
 
+def scaled(z, sent, scale):
+    column = lax.broadcasted_iota(jnp.int32, (z.rows, z.tile), 1)
+    wide = scale[:, z.ny - 1:z.ny]
+    for source in reversed(range(z.ny - 1)):
+        wide = jnp.where(column < (source + 1) * z.cols, scale[:, source:source + 1], wide)
+    return sent.astype(F32) * wide
+
+
 def build(mesh, z):
     def step(student, teacher, bw_table, bw_index, group_ids):
-        each = jnp.arange(z.groups, dtype=group_ids.dtype)
-        largest = jnp.max(jnp.sum((group_ids[None, :] == each[:, None]).astype(jnp.int32), axis=1))
+        sent, scale, loss, largest = sorted_path(z, student, teacher, bw_table, bw_index, group_ids)
         return lax.cond(
             largest <= z.most,
-            functools.partial(sorted_path, z),
-            functools.partial(dense_path, z),
-            student, teacher, bw_table, bw_index, group_ids)
+            lambda *held: (scaled(z, held[0], held[1]), held[2]),
+            lambda *held: dense_path(z, *held[3:]),
+            sent, scale, loss, student, teacher, bw_table, bw_index, group_ids)
 
     return jax.shard_map(
         step, mesh=mesh,

time: 103 us -> 89.9 us (0.87)
  Pallas kernels: 96.5 us -> 83.2 us
    pallas_call x1, Pallas kernels: 96.5 us -> 83.2 us  [sorted_path(): pl.pallas_call(functools.partial(fused, z, ids), out_shape=(jax.ShapeDtyp...]
    mul x0 -> x1, other arithmetic: none -> 1.75 us  [scaled(): return sent.astype(F32) * wide]
where the time goes in v3:
time: 89.9 us; the launch traced here: 89.7 us
  Pallas kernels  83.2 us (93%)
  between operations  2.47 us (3%)
  other arithmetic  1.77 us (2%)
  local copies, waits for them, and re-layouts  1.3 us (1%)
  loops' own time  0.93 us (1%)
    pallas_call x1, Pallas kernels, sorted_path(): pl.pallas_call(functools.partial(fused, z, ids), out_shape=(jax.ShapeDtyp...  83.2 us

profile of v3, /device:TPU:1, one launch (start us, length us, event | category | flops | bytes accessed | tf_op | source)
XLA Modules:
  0.0 89.7 jit_solution(2929389280860296432)
XLA Ops:
  0.6 83.2 %grouped.1 = (s16[384,1024]{1,0:T(8,128)(2,1)}, f32[384,128]{1,0:T(8,128)S(1)}, f32[1,1]{1,0:T(1,128)}, s32[1,1]{1,0:T(1,128)}) custom-call(bf16[384,1024]{1,0:T(8,128)(2,1)} %s_ref.1, bf16[384,1024]{1,0:T(8,128)(2,1)} %t_ref.1, s32[1536]{0:T(1024)} %g_ref.1, f32[8]{0:T(128)} %tab_ref.1, s32[4]{0:T(128)} %idx_ref.1), custom_call_target="tpu_custom_call" | custom-call | tf_op jit(solution)/shard_map/grouped/pallas_call | solution.py:500
  84.6 2.9 %conditional.1 = (f32[384,1024]{1,0:T(8,128)S(1)}, f32[]{:T(128)}) conditional(s32[]{:T(128)} %bitcast.17, (bf16[384,1024]{1,0:T(8,128)(2,1)}, s32[1536]{0:T(1024)}, bf16[384,1024]{1,0:T(8,128)(2,1)}, s32[4]{0:T(128)}, f32[8]{0:T(128)}) %tuple.15, (s16[384,1024]{1,0:T(8,128)(2,1)}, f32[384,128]{1,0:T(8,128)S(1)}, f32[1,1]{1,0:T(1,128)}) %tuple.39), branch_computations={%region_0.8_spmd, %region_8.9_spmd} | conditional | flops 4906549248 | bytes 310783680 | solution.py:591
  84.8 0.1 copy.11
  85.0 1.8 %select_multiply_fusion = f32[384,1024]{1,0:T(8,128)S(1)} fusion(s16[384,1024]{1,0:T(8,128)(2,1)} %get-tuple-element.22, f32[384]{0:T(512)S(1)} %get-tuple-element.45, f32[384]{0:T(512)S(1)} %get-tuple-element.43, f32[384]{0:T(512)S(1)} %get-tuple-element.44, f32[384]{0:T(512)S(1)} %get-tuple-element.42, pred[1024]{0:T(1024)(128)(4,1)S(1)} %get-tuple-element.50, ...), kind=kLoop, calls=%fused_computation.47 | loop fusion | flops 1966080 | bytes 2368512 | tf_op jit(solution)/shard_map/cond/branch_1_fun/mul | solution.py:585
  87.4 0.0 copy-start.8
  87.4 1.1 %copy-done.8 = f32[384,1024]{1,0:T(8,128)} copy-done((f32[384,1024]{1,0:T(8,128)}, f32[384,1024]{1,0:T(8,128)S(1)}, u32[]{:S(2)}) %copy-start.8) | copy-done | bytes 1572888
  (3 shorter events, 0.0 us)
Async XLA Ops:
  87.4 1.1 %copy-start.8 = (f32[384,1024]{1,0:T(8,128)}, f32[384,1024]{1,0:T(8,128)S(1)}, u32[]{:S(2)}) copy-start(f32[384,1024]{1,0:T(8,128)S(1)} %get-tuple-element.73) | copy-start | bytes 4718596

commit v4 on v3

--- a/solution.py
+++ b/solution.py
@@ -68,7 +68,7 @@
     pool = Pool()
     sizes = {
         "in_s": z.ny, "in_t": z.ny, "core": z.groups // 2, "a1": z.nx, "b1": z.ny, "a2": z.ny, "b2": z.nx, "z3": z.nz,
-        "gz": z.nz, "g2a": z.ny, "g2b": z.nx, "g1a": z.nx, "g1b": z.ny, "gc": 1, "out": z.ny, "scale": z.ny, "own": 3,
+        "gz": z.nz, "g2a": z.ny, "g2b": z.nx, "g1a": z.nx, "g1b": z.ny, "gc": 2, "out": z.ny, "scale": z.ny, "own": 3,
     }
     return {name: pool.pair(count) for name, count in sizes.items()}, pool.total
 
@@ -100,6 +100,7 @@
     def on_z(k):
         return lax.rem(zc + k, z.nz)
 
+    z_order = sorted(range(1, z.nz), key=lambda k: -min(k, z.nz - k))
     barrier = pltpu.get_barrier_semaphore()
     peers = [at(yy=on_y(k)) for k in range(1, z.ny)] + [at(xx=on_x(k)) for k in range(1, z.nx)]
     peers += [at(zz=on_z(k)) for k in range(1, z.nz)] + [at(cc=other)]
@@ -314,7 +315,7 @@
     def z3_copy(k, source):
         return copy("z3", u_ref.at[on_z(k)], r3.at[source], k, source, at(zz=on_z(k)))
 
-    for k in range(1, z.nz):
+    for k in z_order:
         z3_copy(k, zc).start()
         pending.append(z3_copy(k, zc))
 
@@ -361,7 +362,7 @@
         one.start()
         pending.append(one)
 
-    for k in range(1, z.nz):
+    for k in z_order:
         start(gz_copy(k, zc))
     for k in range(1, z.nz):
         gz_copy(k, on_z(z.nz - k)).wait_recv()
@@ -394,16 +395,16 @@
         g2b_copy(k, on_x(z.nx - k)).wait_recv()
     for k in range(1, z.ny):
         start(g1b_copy(k, y))
+    def gc_copy(way_of, core):
+        place = wf.at[pl.ds(core * hg + way_of * z.nx, z.nx)]
+        return copy("gc", place, place, way_of, way_of, at(cc=other))
+
     for k in range(1, z.nx):
         g1a_copy(k, on_x(z.nx - k)).wait_recv()
+    start(gc_copy(0, c))
     for k in range(1, z.ny):
         g1b_copy(k, on_y(z.ny - k)).wait_recv()
-
-    def gc_copy(core):
-        place = wf.at[pl.ds(core * hg, hg)]
-        return copy("gc", place, place, 0, 0, at(cc=other))
-
-    start(gc_copy(c))
+    start(gc_copy(1, c))
 
     last = lax.broadcasted_iota(jnp.int32, (z.cap, z.cap), 1) >= z.most
 
@@ -428,17 +429,14 @@
             fs[rows, 0:z.cols] = high
             fs[rows, z.cols:2 * z.cols] = low
 
-    def own_force(i, _):
-        force_of([c * hg + TOGETHER * i + n for n in range(TOGETHER)])
-        return 0
-
-    def other_force(i, _):
-        force_of([other * hg + TOGETHER * i + n for n in range(TOGETHER)])
-        return 0
-
-    lax.fori_loop(0, hg // TOGETHER, own_force, 0)
-    gc_copy(other).wait_recv()
-    lax.fori_loop(0, hg // TOGETHER, other_force, 0)
+    def forces(first):
+        force_of([first + n for n in range(z.nx)])
+
+    forces(c * hg)
+    forces(c * hg + z.nx)
+    for way_of in range(2):
+        gc_copy(way_of, other).wait_recv()
+        forces(other * hg + way_of * z.nx)
 
     l_ref[...] = jnp.sum(jnp.sum(losses[...], axis=0), axis=1, keepdims=True) / z.samples
 
@@ -574,7 +572,7 @@
     pulled = row_wide * pull
     pulled = pulled + jnp.dot(weight_self, students, preferred_element_type=F32)
     pulled = pulled - jnp.dot(weight_cross, teachers, preferred_element_type=F32)
-    return pulled / sizes, loss
+    return unscaled(z, pulled / sizes) + (loss,)
 
 
 def scaled(z, sent, scale):
@@ -585,14 +583,23 @@
     return sent.astype(F32) * wide
 
 
+def unscaled(z, force):
+    parts = force.reshape(z.rows, z.ny, z.cols)
+    top = jnp.maximum(jnp.max(jnp.abs(parts), axis=2, keepdims=True), 1e-33)
+    sent = jnp.round(parts * (32767.0 / top)).astype(jnp.int32).astype(jnp.int16)
+    return sent.reshape(z.rows, z.tile), jnp.pad(top[:, :, 0] / 32767.0, ((0, 0), (0, 128 - z.ny)))
+
+
 def build(mesh, z):
     def step(student, teacher, bw_table, bw_index, group_ids):
         sent, scale, loss, largest = sorted_path(z, student, teacher, bw_table, bw_index, group_ids)
-        return lax.cond(
+        sent, scale, loss = lax.cond(
             largest <= z.most,
-            lambda *held: (scaled(z, held[0], held[1]), held[2]),
+            lambda *held: held[:3],
             lambda *held: dense_path(z, *held[3:]),
             sent, scale, loss, student, teacher, bw_table, bw_index, group_ids)
+        sent, scale, loss = lax.optimization_barrier((sent, scale, loss))
+        return scaled(z, sent, scale), loss
 
     return jax.shard_map(
         step, mesh=mesh,

time: 89.9 us -> 89.6 us (level)
  other arithmetic: 1.77 us -> 2.91 us
    mul x1, other arithmetic: 1.75 us -> 2.89 us  [scaled(): return sent.astype(F32) * wide]
    unnamed x2 -> x0, local copies, waits for them, and re-layouts: 1.14 us -> none
where the time goes in v4:
time: 89.6 us; the launch traced here: 89.4 us
  Pallas kernels  82.7 us (92%)
  other arithmetic  2.91 us (3%)
  between operations  2.48 us (3%)
  loops' own time  0.9 us (1%)
    pallas_call x1, Pallas kernels, sorted_path(): pl.pallas_call(functools.partial(fused, z, ids), out_shape=(jax.ShapeDtyp...  82.7 us
    mul x1, other arithmetic, scaled(): return sent.astype(F32) * wide  2.89 us

profile of v4, /device:TPU:1, one launch (start us, length us, event | category | flops | bytes accessed | tf_op | source)
XLA Modules:
  0.0 89.4 jit_solution(11230994702431085004)
XLA Ops:
  0.6 82.7 %grouped.1 = (s16[384,1024]{1,0:T(8,128)(2,1)}, f32[384,128]{1,0:T(8,128)S(1)}, f32[1,1]{1,0:T(1,128)}, s32[1,1]{1,0:T(1,128)}) custom-call(bf16[384,1024]{1,0:T(8,128)(2,1)} %s_ref.1, bf16[384,1024]{1,0:T(8,128)(2,1)} %t_ref.1, s32[1536]{0:T(1024)} %g_ref.1, f32[8]{0:T(128)} %tab_ref.1, s32[4]{0:T(128)} %idx_ref.1), custom_call_target="tpu_custom_call" | custom-call | tf_op jit(solution)/shard_map/grouped/pallas_call | solution.py:498
  84.0 0.9 %conditional.1 = ((s16[384,1024]{1,0:T(8,128)(2,1)}, f32[384,128]{1,0:T(8,128)S(1)}, f32[]{:T(128)})) conditional(s32[]{:T(128)} %bitcast.16, (bf16[384,1024]{1,0:T(8,128)(2,1)}, s32[1536]{0:T(1024)}, bf16[384,1024]{1,0:T(8,128)(2,1)}, s32[4]{0:T(128)}, f32[8]{0:T(128)}) %tuple.15, (s16[384,1024]{1,0:T(8,128)(2,1)}, f32[384,128]{1,0:T(8,128)S(1)}, ...), branch_computations={%region_0.9_spmd, %region_9.10_spmd} | conditional | flops 4908911616 | bytes 335396640 | solution.py:596
  84.9 0.5 slice_reduce_fusion.3
  85.4 2.9 %select_multiply_fusion = f32[384,1024]{1,0:T(8,128)} fusion(s16[384,1024]{1,0:T(8,128)(2,1)} %get-tuple-element.34, f32[384]{0:T(512)S(1)} %get-tuple-element.40, f32[384]{0:T(512)S(1)} %get-tuple-element.41, f32[384]{0:T(512)S(1)} %get-tuple-element.42, f32[384]{0:T(512)S(1)} %get-tuple-element.39, pred[1024]{0:T(1024)(128)(4,1)S(1)} %get-tuple-element.59, ...), kind=kLoop, calls=%fused_computation.50 | loop fusion | flops 1966080 | bytes 2368512 | tf_op jit(solution)/shard_map/mul | solution.py:583
  (2 shorter events, 0.0 us)

commit v5 on v4

v5 whole, which is shorter than its diff:
```python
import functools

import jax
import jax.numpy as jnp
from jax import lax
from jax.experimental import pallas as pl
from jax.experimental.pallas import tpu as pltpu
from jax.sharding import PartitionSpec as P

MESH = pl.DeviceIdType.MESH
F32, BF16 = jnp.float32, jnp.bfloat16


TOGETHER = 4


class Sizes:
    def __init__(self, ny, nx, nz, nc, samples, tile, latent):
        self.ny, self.nx, self.nz, self.nc = ny, nx, nz, nc
        self.samples, self.tile, self.latent = samples, tile, float(latent)
        self.rows = samples // ny
        self.cols = tile // ny
        self.groups = 2 * nc * nx
        self.half = nz // 2
        self.cap = 8 * ny * self.half
        self.blocks = self.cap // 8
        self.most = self.cap - 3
        self.lanes = min(128, self.rows)


def pair_terms(dist_self, dist_cross, mask, heights, latent):
    kern_self = jnp.zeros_like(dist_self)
    kern_cross = jnp.zeros_like(dist_cross)
    weight_self = jnp.zeros_like(dist_self)
    weight_cross = jnp.zeros_like(dist_cross)
    count = len(heights)
    for height in heights:
        width_now = height * latent
        exp_self = jnp.exp(-dist_self / width_now)
        exp_cross = jnp.exp(-dist_cross / width_now)
        kern_self = kern_self + exp_self
        kern_cross = kern_cross + exp_cross
        weight_self = weight_self + exp_self / height
        weight_cross = weight_cross + exp_cross / height
    kern_self = kern_self / count * mask
    kern_cross = kern_cross / count * mask
    weight_self = weight_self / count * mask
    weight_cross = weight_cross / count * mask
    row_loss = jnp.sum(kern_self - 2.0 * kern_cross, axis=1, keepdims=True)
    pull = jnp.sum(weight_cross, axis=1, keepdims=True) - jnp.sum(weight_self, axis=1, keepdims=True)
    return weight_self.astype(BF16), weight_cross.astype(BF16), row_loss, pull


class Pool:
    def __init__(self):
        self.total = 0

    def take(self, count):
        first = self.total
        self.total += count
        return first

    def pair(self, count):
        return self.take(count), self.take(count)


def exchanges(z):
    pool = Pool()
    sizes = {
        "in_s": z.ny, "in_t": z.ny, "core_s": z.groups // 2, "core_c": z.groups // 2, "s1a": z.nx, "s1b": z.nx, "s2a": z.ny, "s2b": z.ny, "s3": z.nz,
        "a1": z.nx, "b1": z.ny, "a2": z.ny, "b2": z.nx, "z3": z.nz,
        "gz": z.nz, "g2a": z.ny, "g2b": z.nx, "g1a": z.nx, "g1b": z.ny, "gc": 2, "out": z.ny, "scale": z.ny, "own": 3,
    }
    return {name: pool.pair(count) for name, count in sizes.items()}, pool.total


def fused(z, ids, s_ref, t_ref, g_ref, tab_ref, idx_ref, f_ref, l_ref, most_ref,
          xin_s, xin_t, sort_ref, back_ref, xacc, xs, norms, ds_ref, dc_ref, rc_s, rc_c, r1sa, r1sb, r2sa, r2sb, sum_sa, sum_sb,
          us_ref, r3s, r1a, r1b, sums, r2a, r2b, u_ref, r3, wf, gr_ref, row_place, col_place, losses, fs, qs, ql, scales, landed, sems):
    y, v = lax.axis_index("pair"), lax.axis_index("value")
    c = lax.rem(v, z.nc)
    x = lax.rem(v // z.nc, z.nx)
    zc = v // (z.nc * z.nx)
    other = 1 - c
    hg = z.groups // 2
    quarter = z.cap // z.ny

    def at(yy=None, xx=None, zz=None, cc=None):
        yy = y if yy is None else yy
        xx = x if xx is None else xx
        zz = zc if zz is None else zz
        cc = c if cc is None else cc
        return (yy, (zz * z.nx + xx) * z.nc + cc)

    def on_y(k):
        return lax.rem(y + k, z.ny)

    def on_x(k):
        return lax.rem(x + k, z.nx)

    def on_z(k):
        return lax.rem(zc + k, z.nz)

    z_order = sorted(range(1, z.nz), key=lambda k: -min(k, z.nz - k))
    barrier = pltpu.get_barrier_semaphore()
    peers = [at(yy=on_y(k)) for k in range(1, z.ny)] + [at(xx=on_x(k)) for k in range(1, z.nx)]
    peers += [at(zz=on_z(k)) for k in range(1, z.nz)] + [at(cc=other)]
    for peer in peers:
        pl.semaphore_signal(barrier, inc=1, device_id=peer, device_id_type=MESH)
    pl.semaphore_wait(barrier, len(peers))

    def copy(name, src, dst, send, recv, device):
        first_send, first_recv = ids[name]
        return pltpu.make_async_remote_copy(
            src_ref=src, dst_ref=dst, send_sem=sems.at[first_send + send], recv_sem=sems.at[first_recv + recv],
            device_id=device, device_id_type=MESH)

    pending = []

    def drain():
        for one in pending:
            one.wait_send()

    order = sorted(range(1, z.ny), key=lambda k: min(k, z.ny - k))

    def in_copy(name, ref, land, k, source, target):
        cols = pl.ds(pl.multiple_of(target * z.cols, z.cols), z.cols)
        return copy(name, ref.at[:, cols], land.at[source], k, source, at(yy=on_y(k)))

    for k in order:
        in_copy("in_s", s_ref, xin_s, k, y, on_y(k)).start()
        pending.append(in_copy("in_t", t_ref, xin_t, k, y, on_y(k)))
    own_cols = pl.ds(pl.multiple_of(y * z.cols, z.cols), z.cols)
    own_s = pltpu.make_async_copy(s_ref.at[:, own_cols], xin_s.at[y], sems.at[ids["own"][0]])
    own_t = pltpu.make_async_copy(t_ref.at[:, own_cols], xin_t.at[y], sems.at[ids["own"][0] + 1])
    own_s.start()
    own_t.start()

    gr_ref[...] = g_ref[...].reshape(1, z.samples)
    slots = z.groups * z.cap
    eye = lax.broadcasted_iota(jnp.int32, (z.cap, z.cap), 0) == lax.broadcasted_iota(jnp.int32, (z.cap, z.cap), 1)
    above = lax.broadcasted_iota(jnp.int32, (z.cap, z.cap), 0) < lax.broadcasted_iota(jnp.int32, (z.cap, z.cap), 1)
    above = jnp.where(above, 1.0, 0.0).astype(BF16)

    def find_places(step, seen):
        first = pl.multiple_of(step * z.cap, z.cap)
        ids_row = gr_ref[:, pl.ds(first, z.cap)]
        hit = jnp.where(lax.broadcasted_iota(jnp.int32, (z.groups, z.cap), 0) == ids_row, 1.0, 0.0)
        before = seen + jnp.dot(hit.astype(BF16), above, preferred_element_type=F32)
        place = (ids_row * z.cap).astype(F32) + jnp.sum(hit * before, axis=0, keepdims=True)
        row_place[:, pl.ds(first, z.cap)] = place.astype(jnp.int32)
        turned = jnp.sum(jnp.where(eye, place, 0.0), axis=1, keepdims=True)
        col_place[pl.ds(first, z.cap), :] = turned.astype(jnp.int32)
        return seen + jnp.sum(hit, axis=1, keepdims=True)

    held = lax.fori_loop(0, z.samples // z.cap, find_places, jnp.zeros((z.groups, 1), F32))
    most_ref[...] = jnp.max(held, axis=0, keepdims=True).astype(jnp.int32)

    for part in range(z.ny):
        def fill_sort(step, _):
            first = pl.multiple_of(step * z.cap, z.cap)
            slot = first + lax.broadcasted_iota(jnp.int32, (z.cap, z.rows), 0)
            place = row_place[:, part * z.rows:(part + 1) * z.rows]
            sort_ref[part, pl.ds(first, z.cap), :] = jnp.where(slot == place, 1.0, 0.0).astype(BF16)
            return 0

        lax.fori_loop(0, z.groups, fill_sort, 0)

    for k in order:
        in_copy("in_s", s_ref, xin_s, k, y, on_y(k)).wait_send()
        in_copy("in_t", t_ref, xin_t, k, y, on_y(k)).start()

    own_s.wait()
    own_t.wait()
    xacc[...] = jnp.zeros_like(xacc)
    tall_rows = slots // 4

    def sort_from(source, values, first_col):
        def body(step, _):
            first = pl.multiple_of(step * tall_rows, tall_rows)
            place = sort_ref[source, pl.ds(first, tall_rows), :]
            xacc[pl.ds(first, tall_rows), first_col:first_col + z.cols] += jnp.dot(
                place, values[source], preferred_element_type=F32)
            return 0

        lax.fori_loop(0, 4, body, 0)

    sort_from(y, xin_s, 0)
    for k in order:
        source = on_y(z.ny - k)
        in_copy("in_s", s_ref, xin_s, k, source, on_y(k)).wait_recv()
        sort_from(source, xin_s, 0)

    def rows_of(group):
        return pl.ds(pl.multiple_of(group * z.cap, z.cap), z.cap)

    outer = (((1,), (1,)), ((), ()))

    def distances_self(groups):
        found = []
        for group in groups:
            mine = xacc[rows_of(group), 0:z.cols].astype(BF16)
            found.append((mine, lax.dot_general(mine, mine, outer, preferred_element_type=F32)))
        parts = []
        for mine, gram in found:
            diagonal = jnp.where(eye, gram, 0.0)
            norm_col = jnp.sum(diagonal, axis=1, keepdims=True)
            parts.append((norm_col, norm_col + jnp.sum(diagonal, axis=0, keepdims=True) - 2.0 * gram))
        for group, (mine, _), (norm_col, part) in zip(groups, found, parts):
            xs[group, 0:z.cap] = mine
            norms[group] = norm_col
            ds_ref[group] = part

    def distances_cross(groups):
        found = []
        for group in groups:
            theirs = xacc[rows_of(group), z.cols:2 * z.cols].astype(BF16)
            both = jnp.concatenate([xs[group, 0:z.cap], theirs], axis=0)
            found.append((theirs, lax.dot_general(both, theirs, outer, preferred_element_type=F32)))
        parts = []
        for group, (theirs, gram) in zip(groups, found):
            norm_row = jnp.sum(jnp.where(eye, gram[z.cap:2 * z.cap], 0.0), axis=0, keepdims=True)
            parts.append(norms[group] + norm_row - 2.0 * gram[0:z.cap])
        for group, (theirs, _), part in zip(groups, found, parts):
            xs[group, z.cap:2 * z.cap] = theirs
            dc_ref[group] = part

    def core_copy(name, part, land, i, group):
        return copy(name, part.at[group], land.at[i], i, i, at(cc=other))

    def quarter_of(k):
        return pl.ds(pl.multiple_of(k * quarter, quarter), quarter)

    def self_to_other(i, _):
        now = [TOGETHER * i + n for n in range(TOGETHER)]
        distances_self([other * hg + n for n in now])
        for n in now:
            core_copy("core_s", ds_ref, rc_s, n, other * hg + n).start()
        return 0

    lax.fori_loop(0, hg // TOGETHER, self_to_other, 0)

    def self_mine(i, _):
        now = [TOGETHER * i + n for n in range(TOGETHER)]
        distances_self([c * hg + n for n in now])
        for n in now:
            core_copy("core_s", ds_ref, rc_s, n, c * hg + n).wait_recv()
            ds_ref[c * hg + n] += rc_s[n]
        return 0

    lax.fori_loop(0, hg // TOGETHER, self_mine, 0)

    def s1_copies(k, source):
        second = ds_ref.at[pl.ds(c * hg + z.nx, z.nx), quarter_of(on_x(k))]
        return (copy("s1a", ds_ref.at[c * hg + on_x(k)], r1sa.at[source], k, source, at(xx=on_x(k))),
                copy("s1b", second, r1sb.at[source], k, source, at(xx=on_x(k))))

    def start(*copies):
        for one in copies:
            one.start()
            pending.append(one)

    for k in range(1, z.nx):
        start(*s1_copies(k, x))
    for i in range(hg):
        pending.append(core_copy("core_s", ds_ref, rc_s, i, other * hg + i))

    def fill_back(step, _):
        first = pl.multiple_of(step * z.cap, z.cap)
        slot = lax.broadcasted_iota(jnp.int32, (z.cap, slots), 1)
        back_ref[pl.ds(first, z.cap), :] = jnp.where(slot == col_place[pl.ds(first, z.cap), :], 1.0, 0.0).astype(BF16)
        return 0

    lax.fori_loop(0, z.samples // z.cap, fill_back, 0)

    sort_from(y, xin_t, z.cols)
    for k in order:
        source = on_y(z.ny - k)
        in_copy("in_t", t_ref, xin_t, k, source, on_y(k)).wait_recv()
        sort_from(source, xin_t, z.cols)

    def cross_to_other(i, _):
        now = [TOGETHER * i + n for n in range(TOGETHER)]
        distances_cross([other * hg + n for n in now])
        for n in now:
            core_copy("core_c", dc_ref, rc_c, n, other * hg + n).start()
        return 0

    lax.fori_loop(0, hg // TOGETHER, cross_to_other, 0)

    def a1_copy(k, source):
        return copy("a1", dc_ref.at[c * hg + on_x(k)], r1a.at[source], k, source, at(xx=on_x(k)))

    def b1_copy(k, source):
        return copy("b1", dc_ref.at[c * hg + z.nx + on_y(k)], r1b.at[source], k, source, at(yy=on_y(k)))

    def mine(k, _):
        now = (on_x(k), z.nx + on_y(k))
        distances_cross([c * hg + i for i in now])
        for i in now:
            core_copy("core_c", dc_ref, rc_c, i, c * hg + i).wait_recv()
            dc_ref[c * hg + i] += rc_c[i]

        @pl.when(k < z.nx)
        def _():
            a1_copy(k, x).start()
            b1_copy(k, y).start()

        return 0

    lax.fori_loop(1, z.nx + 1, mine, 0)
    for i in range(hg):
        pending.append(core_copy("core_c", dc_ref, rc_c, i, other * hg + i))
    for k in range(1, z.nx):
        pending.extend([a1_copy(k, x), b1_copy(k, y)])

    total_a = ds_ref[c * hg + x]
    total_b = ds_ref[pl.ds(c * hg + z.nx, z.nx), quarter_of(x), :]
    for k in range(1, z.nx):
        source = on_x(z.nx - k)
        for one in s1_copies(k, source):
            one.wait_recv()
        total_a = total_a + r1sa[source]
        total_b = total_b + r1sb[source]
    sum_sa[...] = total_a
    sum_sb[...] = total_b

    def s2_copies(k, source):
        return (copy("s2a", sum_sa.at[quarter_of(on_y(k))], r2sa.at[source], k, source, at(yy=on_y(k))),
                copy("s2b", sum_sb.at[on_y(k)], r2sb.at[source], k, source, at(yy=on_y(k))))

    for k in range(1, z.ny):
        start(*s2_copies(k, y))
    part_a = sum_sa[quarter_of(y), :]
    part_b = sum_sb[y]
    for k in range(1, z.ny):
        source = on_y(z.ny - k)
        for one in s2_copies(k, source):
            one.wait_recv()
        part_a = part_a + r2sa[source]
        part_b = part_b + r2sb[source]
    us_ref[0:z.half] = part_a.reshape(z.half, 8, z.cap)
    us_ref[z.half:2 * z.half] = part_b.reshape(z.half, 8, z.cap)

    def s3_copy(k, source):
        return copy("s3", us_ref.at[on_z(k)], r3s.at[source], k, source, at(zz=on_z(k)))

    for k in z_order:
        start(s3_copy(k, zc))

    total_a = dc_ref[c * hg + x]
    for k in range(1, z.nx):
        source = on_x(z.nx - k)
        a1_copy(k, source).wait_recv()
        total_a = total_a + r1a[source]
    sums[0] = total_a

    def a2_copy(k, source):
        return copy("a2", sums.at[0, quarter_of(on_y(k))], r2a.at[source], k, source, at(yy=on_y(k)))

    for k in range(1, z.ny):
        start(a2_copy(k, y))
    total_b = dc_ref[c * hg + z.nx + y]
    for k in range(1, z.ny):
        source = on_y(z.ny - k)
        b1_copy(k, source).wait_recv()
        total_b = total_b + r1b[source]
    sums[1] = total_b

    def b2_copy(k, source):
        return copy("b2", sums.at[1, quarter_of(on_x(k))], r2b.at[source], k, source, at(xx=on_x(k)))

    for k in range(1, z.nx):
        start(b2_copy(k, x))

    part_a = sums[0, quarter_of(y), :]
    for k in range(1, z.ny):
        source = on_y(z.ny - k)
        a2_copy(k, source).wait_recv()
        part_a = part_a + r2a[source]
    u_ref[0:z.half] = part_a.reshape(z.half, 8, z.cap)
    part_b = sums[1, quarter_of(x), :]
    for k in range(1, z.nx):
        source = on_x(z.nx - k)
        b2_copy(k, source).wait_recv()
        part_b = part_b + r2b[source]
    u_ref[z.half:2 * z.half] = part_b.reshape(z.half, 8, z.cap)

    def z3_copy(k, source):
        return copy("z3", u_ref.at[on_z(k)], r3.at[source], k, source, at(zz=on_z(k)))

    for k in z_order:
        start(z3_copy(k, zc))
    dist_self = us_ref[zc]
    for k in range(1, z.nz):
        source = on_z(z.nz - k)
        s3_copy(k, source).wait_recv()
        dist_self = dist_self + r3s[source]
    dist_cross = u_ref[zc]
    for k in range(1, z.nz):
        source = on_z(z.nz - k)
        z3_copy(k, source).wait_recv()
        dist_cross = dist_cross + r3[source]

    way = zc // z.half
    member = (1 - way) * x + way * y
    sub = (1 - way) * y + way * x
    group = c * hg + way * z.nx + member
    block = sub * z.half + lax.rem(zc, z.half)
    size = jnp.sum(jnp.where(gr_ref[...] == group, 1.0, 0.0), axis=1, keepdims=True)
    row_at = (block * 8 + lax.broadcasted_iota(jnp.int32, (8, z.cap), 0)).astype(F32)
    col_at = lax.broadcasted_iota(jnp.int32, (8, z.cap), 1).astype(F32)
    mask = jnp.where((row_at < size) & (col_at < size), 1.0, 0.0)
    heights = [tab_ref[idx_ref[m]] for m in range(4)]
    weight_self, weight_cross, row_loss, pull = pair_terms(
        jnp.maximum(dist_self, 0.0), jnp.maximum(dist_cross, 0.0), mask, heights, z.latent)
    lanes = lax.broadcasted_iota(jnp.int32, (8, z.cap), 1)

    def with_row_term(weights, term):
        first = term.astype(BF16).astype(F32)
        second = (term - first).astype(BF16).astype(F32)
        third = term - first - second
        columns = jnp.where(lanes == z.cap - 3, first, jnp.where(lanes == z.cap - 2, second, third))
        return jnp.where(lanes < z.most, weights, columns)

    wf[group, block] = jnp.concatenate(
        [with_row_term(weight_self.astype(F32), pull), with_row_term(-weight_cross.astype(F32), row_loss / size)],
        axis=0).astype(BF16)

    def gz_copy(k, source):
        way_of = source // z.half
        group_of = c * hg + way_of * z.nx + (1 - way_of) * x + way_of * y
        block_of = ((1 - way_of) * y + way_of * x) * z.half + lax.rem(source, z.half)
        place = wf.at[group_of, block_of]
        return copy("gz", place, place, k, source, at(zz=on_z(k)))

    for k in z_order:
        start(gz_copy(k, zc))
    for k in range(1, z.nz):
        gz_copy(k, on_z(z.nz - k)).wait_recv()

    def g2a_copy(k, source):
        place = wf.at[c * hg + x, pl.ds(source * z.half, z.half)]
        return copy("g2a", place, place, k, source, at(yy=on_y(k)))

    def g2b_copy(k, source):
        place = wf.at[c * hg + z.nx + y, pl.ds(source * z.half, z.half)]
        return copy("g2b", place, place, k, source, at(xx=on_x(k)))

    for k in range(1, z.nx):
        start(g2a_copy(k, y))
        start(g2b_copy(k, x))

    def g1a_copy(k, source):
        place = wf.at[c * hg + source]
        return copy("g1a", place, place, k, source, at(xx=on_x(k)))

    def g1b_copy(k, source):
        place = wf.at[c * hg + z.nx + source]
        return copy("g1b", place, place, k, source, at(yy=on_y(k)))

    for k in range(1, z.ny):
        g2a_copy(k, on_y(z.ny - k)).wait_recv()
    for k in range(1, z.nx):
        start(g1a_copy(k, x))
    for k in range(1, z.nx):
        g2b_copy(k, on_x(z.nx - k)).wait_recv()
    for k in range(1, z.ny):
        start(g1b_copy(k, y))
    def gc_copy(way_of, core):
        place = wf.at[pl.ds(core * hg + way_of * z.nx, z.nx)]
        return copy("gc", place, place, way_of, way_of, at(cc=other))

    for k in range(1, z.nx):
        g1a_copy(k, on_x(z.nx - k)).wait_recv()
    start(gc_copy(0, c))
    for k in range(1, z.ny):
        g1b_copy(k, on_y(z.ny - k)).wait_recv()
    start(gc_copy(1, c))

    last = lax.broadcasted_iota(jnp.int32, (z.cap, z.cap), 1) >= z.most

    def force_of(groups):
        found = []
        for g in groups:
            held = wf[g].astype(F32).reshape(z.blocks, 2, 8, z.cap)
            to_self, to_cross = held[:, 0].reshape(z.cap, z.cap), held[:, 1].reshape(z.cap, z.cap)
            pulls = jnp.sum(jnp.where(last, to_self, 0.0), axis=1, keepdims=True)
            loss = jnp.sum(jnp.where(last, to_cross, 0.0), axis=0, keepdims=True)
            weights = jnp.concatenate([to_self, to_cross], axis=1).astype(BF16)
            values = xs[g]
            pulled = values[0:z.cap].astype(F32) * pulls + jnp.dot(weights, values, preferred_element_type=F32)
            size_of = jnp.sum(jnp.where(gr_ref[...] == g, 1.0, 0.0), axis=1, keepdims=True)
            force = pulled / size_of
            high = force.astype(BF16)
            low = (force - high.astype(F32)).astype(BF16)
            found.append((loss, high, low))
        for g, (loss, high, low) in zip(groups, found):
            rows = pl.ds(pl.multiple_of(g * z.cap, z.cap), z.cap)
            losses[g] = loss
            fs[rows, 0:z.cols] = high
            fs[rows, z.cols:2 * z.cols] = low

    def forces(first):
        force_of([first + n for n in range(z.nx)])

    forces(c * hg)
    forces(c * hg + z.nx)
    for way_of in range(2):
        gc_copy(way_of, other).wait_recv()
        forces(other * hg + way_of * z.nx)

    l_ref[...] = jnp.sum(jnp.sum(losses[...], axis=0), axis=1, keepdims=True) / z.samples

    def out_copies(k, source):
        return (copy("out", qs.at[k], ql.at[source], k, source, at(yy=on_y(k))),
                copy("scale", scales.at[k], landed.at[source], k, source, at(yy=on_y(k))))

    parts = z.rows // z.lanes
    square = (z.lanes, z.lanes)
    same = lax.broadcasted_iota(jnp.int32, square, 0) == lax.broadcasted_iota(jnp.int32, square, 1)

    def unsorted(k):
        rows = pl.ds(pl.multiple_of(on_y(k) * z.rows, z.rows), z.rows)
        moved = jnp.dot(back_ref[rows, :], fs[...], preferred_element_type=F32)
        return moved[:, 0:z.cols] + moved[:, z.cols:2 * z.cols]

    def send_out(step, _):
        k = lax.rem(step + z.ny // 2 - 1, z.ny - 1) + 1
        force = unsorted(k)
        top = jnp.maximum(jnp.max(jnp.abs(force), axis=1, keepdims=True), 1e-33)
        qs[k] = jnp.round(force * (32767.0 / top)).astype(jnp.int32).astype(jnp.int16)
        unit = top / 32767.0
        for part in range(parts):
            spread = jnp.where(same, unit[part * z.lanes:(part + 1) * z.lanes], 0.0)
            scales[k, part:part + 1, :] = jnp.sum(spread, axis=0, keepdims=True)
        for one in out_copies(k, y):
            one.start()
        return 0

    scales[...] = jnp.zeros_like(scales)
    lax.fori_loop(0, z.ny - 1, send_out, 0)
    f_ref[:, own_cols] = unsorted(0)
    for k in order:
        source = on_y(z.ny - k)
        for one in out_copies(k, source):
            one.wait_recv()
        cols = pl.ds(pl.multiple_of(source * z.cols, z.cols), z.cols)
        for part in range(parts):
            rows = slice(part * z.lanes, (part + 1) * z.lanes)
            unit = jnp.sum(jnp.where(same, landed[source, part:part + 1, :], 0.0), axis=1, keepdims=True)
            f_ref[rows, cols] = ql[source, rows, :].astype(jnp.int32).astype(F32) * unit

    for k in range(1, z.ny):
        pending += out_copies(k, y)
    drain()


def sorted_path(z, student, teacher, bw_table, bw_index, group_ids):
    ids, count = exchanges(z)
    slots, hg = z.groups * z.cap, z.groups // 2
    quarter = z.cap // z.ny
    vmem, smem, anywhere = (pl.BlockSpec(memory_space=m) for m in (pltpu.VMEM, pltpu.SMEM, pl.ANY))
    force, loss, largest = pl.pallas_call(
        functools.partial(fused, z, ids),
        out_shape=(jax.ShapeDtypeStruct((z.rows, z.tile), F32), jax.ShapeDtypeStruct((1, 1), F32),
                   jax.ShapeDtypeStruct((1, 1), jnp.int32)),
        in_specs=[anywhere, anywhere, vmem, smem, smem],
        out_specs=(vmem, vmem, vmem),
        scratch_shapes=[
            pltpu.VMEM((z.ny, z.rows, z.cols), BF16),
            pltpu.VMEM((z.ny, z.rows, z.cols), BF16),
            pltpu.VMEM((z.ny, slots, z.rows), BF16),
            pltpu.VMEM((z.samples, slots), BF16),
            pltpu.VMEM((slots, 2 * z.cols), F32),
            pltpu.VMEM((z.groups, 2 * z.cap, z.cols), BF16),
            pltpu.VMEM((z.groups, z.cap, 1), F32),
            pltpu.VMEM((z.groups, z.cap, z.cap), F32),
            pltpu.VMEM((z.groups, z.cap, z.cap), F32),
            pltpu.VMEM((hg, z.cap, z.cap), F32),
            pltpu.VMEM((hg, z.cap, z.cap), F32),
            pltpu.VMEM((z.nx, z.cap, z.cap), F32),
            pltpu.VMEM((z.nx, z.nx, quarter, z.cap), F32),
            pltpu.VMEM((z.ny, quarter, z.cap), F32),
            pltpu.VMEM((z.ny, quarter, z.cap), F32),
            pltpu.VMEM((z.cap, z.cap), F32),
            pltpu.VMEM((z.nx, quarter, z.cap), F32),
            pltpu.VMEM((z.nz, 8, z.cap), F32),
            pltpu.VMEM((z.nz, 8, z.cap), F32),
            pltpu.VMEM((z.nx, z.cap, z.cap), F32),
            pltpu.VMEM((z.ny, z.cap, z.cap), F32),
            pltpu.VMEM((2, z.cap, z.cap), F32),
            pltpu.VMEM((z.ny, quarter, z.cap), F32),
            pltpu.VMEM((z.nx, quarter, z.cap), F32),
            pltpu.VMEM((z.nz, 8, z.cap), F32),
            pltpu.VMEM((z.nz, 8, z.cap), F32),
            pltpu.VMEM((z.groups, z.blocks, 16, z.cap), BF16),
            pltpu.VMEM((1, z.samples), jnp.int32),
            pltpu.VMEM((1, z.samples), jnp.int32),
            pltpu.VMEM((z.samples, 1), jnp.int32),
            pltpu.VMEM((z.groups, 1, z.cap), F32),
            pltpu.VMEM((slots, 2 * z.cols), BF16),
            pltpu.VMEM((z.ny, z.rows, z.cols), jnp.int16),
            pltpu.VMEM((z.ny, z.rows, z.cols), jnp.int16),
            pltpu.VMEM((z.ny, 8, z.lanes), F32),
            pltpu.VMEM((z.ny, 8, z.lanes), F32),
            pltpu.SemaphoreType.DMA((count,)),
        ],
        compiler_params=pltpu.CompilerParams(
            collective_id=1, has_side_effects=True, vmem_limit_bytes=56 * 1024 * 1024),
        name="grouped",
    )(student, teacher, group_ids, bw_table, bw_index)
    return force, loss.reshape(()), largest.reshape(())


def gather_pair(z, block):
    y = lax.axis_index("pair")
    out = jnp.zeros((z.ny,) + block.shape, block.dtype)
    for k in range(z.ny):
        moved = lax.ppermute(block, "pair", [(i, (i + k) % z.ny) for i in range(z.ny)]) if k else block
        out = lax.dynamic_update_index_in_dim(out, moved, lax.rem(y + z.ny - k, z.ny), 0)
    return out.reshape((z.ny * block.shape[0],) + block.shape[1:])


def sum_over(array, axis, count):
    step = 1
    while step < count:
        array = array + lax.ppermute(array, axis, [(i, i ^ step) for i in range(count)])
        step *= 2
    return array


def dense_path(z, student, teacher, bw_table, bw_index, group_ids):
    students = gather_pair(z, student)
    teachers = gather_pair(z, teacher)
    both = jnp.concatenate([students, teachers], axis=0)
    wide = both.astype(F32)
    row_wide = student.astype(F32)
    norms = jnp.sum(wide * wide, axis=1)
    row_norms = jnp.sum(row_wide * row_wide, axis=1)
    gram = lax.dot_general(student, both, (((1,), (1,)), ((), ())), preferred_element_type=F32)
    part = row_norms[:, None] + norms[None, :] - 2.0 * gram
    dist = jnp.maximum(sum_over(part, "value", z.nx * z.nz * z.nc), 0.0)
    row_ids = lax.dynamic_slice_in_dim(group_ids, lax.axis_index("pair") * z.rows, z.rows)
    same = (row_ids[:, None] == group_ids[None, :]).astype(F32)
    sizes = jnp.sum(same, axis=1, keepdims=True)
    heights = bw_table[bw_index]
    weight_self, weight_cross, row_loss, pull = pair_terms(
        dist[:, :z.samples], dist[:, z.samples:], same, [heights[m] for m in range(4)], z.latent)
    loss = sum_over(jnp.broadcast_to(jnp.sum(row_loss / sizes), (8, 128)), "pair", z.ny)[0, 0] / z.samples
    pulled = row_wide * pull
    pulled = pulled + jnp.dot(weight_self, students, preferred_element_type=F32)
    pulled = pulled - jnp.dot(weight_cross, teachers, preferred_element_type=F32)
    return pulled / sizes, loss


def build(mesh, z):
    def step(student, teacher, bw_table, bw_index, group_ids):
        force, loss, largest = sorted_path(z, student, teacher, bw_table, bw_index, group_ids)
        return lax.cond(
            largest <= z.most,
            lambda *held: held[:2],
            lambda *held: dense_path(z, *held[2:]),
            force, loss, student, teacher, bw_table, bw_index, group_ids)

    return jax.shard_map(
        step, mesh=mesh,
        in_specs=(P("pair", "value"), P("pair", "value"), P(None), P(None), P(None)),
        out_specs=(P("pair", "value"), P()),
        check_vma=False)


def solution(mesh):
    return build(mesh, Sizes(ny=4, nx=4, nz=8, nc=2, samples=1536, tile=1024, latent=65536))
```

time: 89.6 us -> 89 us (level)
  other arithmetic: 2.91 us -> 0 us
  local copies, waits for them, and re-layouts: 0.46 us -> 2.73 us
    mul x1 -> x0, other arithmetic: 2.89 us -> none  [scaled(): return sent.astype(F32) * wide]
    unnamed x0 -> x1, local copies, waits for them, and re-layouts: none -> 2.73 us
where the time goes in v5:
time: 89 us; the launch traced here: 88.9 us
  Pallas kernels  82.9 us (93%)
  local copies, waits for them, and re-layouts  2.73 us (3%)
  between operations  2.33 us (3%)
    pallas_call x1, Pallas kernels, sorted_path(): pl.pallas_call(functools.partial(fused, z, ids), out_shape=(jax.ShapeDtyp...  82.9 us
    unnamed x1, local copies, waits for them, and re-layouts  2.73 us

profile of v5, /device:TPU:1, one launch (start us, length us, event | category | flops | bytes accessed | tf_op | source)
XLA Modules:
  0.0 88.9 jit_solution(92899400949055205)
XLA Ops:
  0.6 82.9 %grouped.1 = (f32[384,1024]{1,0:T(8,128)}, f32[1,1]{1,0:T(1,128)}, s32[1,1]{1,0:T(1,128)}) custom-call(bf16[384,1024]{1,0:T(8,128)(2,1)} %s_ref.1, bf16[384,1024]{1,0:T(8,128)(2,1)} %t_ref.1, s32[1536]{0:T(1024)} %g_ref.1, f32[8]{0:T(128)} %tab_ref.1, s32[4]{0:T(128)} %idx_ref.1), custom_call_target="tpu_custom_call" | custom-call | tf_op jit(solution)/shard_map/grouped/pallas_call | solution.py:564
  84.1 0.9 conditional.1
  85.0 2.7 %copy.25 = f32[384,1024]{1,0:T(8,128)} copy(f32[384,1024]{1,0:T(8,128)} %get-tuple-element.62) | data formatting | bytes 3145728

commit v6 on v5

--- a/solution.py
+++ b/solution.py
@@ -12,6 +12,7 @@
 
 
 TOGETHER = 4
+STEPS = 32767.0
 
 
 class Sizes:
@@ -69,14 +70,14 @@
     sizes = {
         "in_s": z.ny, "in_t": z.ny, "core_s": z.groups // 2, "core_c": z.groups // 2, "s1a": z.nx, "s1b": z.nx, "s2a": z.ny, "s2b": z.ny, "s3": z.nz,
         "a1": z.nx, "b1": z.ny, "a2": z.ny, "b2": z.nx, "z3": z.nz,
-        "gz": z.nz, "g2a": z.ny, "g2b": z.nx, "g1a": z.nx, "g1b": z.ny, "gc": 2, "out": z.ny, "scale": z.ny, "own": 3,
+        "gz": z.nz, "g2a": z.ny, "g2b": z.nx, "g1a": z.nx, "g1b": z.ny, "gc": 2, "out": z.ny, "scale": z.ny, "own": 2 + z.ny,
     }
     return {name: pool.pair(count) for name, count in sizes.items()}, pool.total
 
 
 def fused(z, ids, s_ref, t_ref, g_ref, tab_ref, idx_ref, f_ref, l_ref, most_ref,
           xin_s, xin_t, sort_ref, back_ref, xacc, xs, norms, ds_ref, dc_ref, rc_s, rc_c, r1sa, r1sb, r2sa, r2sb, sum_sa, sum_sb,
-          us_ref, r3s, r1a, r1b, sums, r2a, r2b, u_ref, r3, wf, gr_ref, row_place, col_place, losses, fs, qs, ql, scales, landed, sems):
+          us_ref, r3s, r1a, r1b, sums, r2a, r2b, u_ref, r3, wf, gr_ref, row_place, col_place, sizes, losses, fs, qs, ql, fo, scales, landed, sems):
     y, v = lax.axis_index("pair"), lax.axis_index("value")
     c = lax.rem(v, z.nc)
     x = lax.rem(v // z.nc, z.nx)
@@ -154,6 +155,7 @@
         return seen + jnp.sum(hit, axis=1, keepdims=True)
 
     held = lax.fori_loop(0, z.samples // z.cap, find_places, jnp.zeros((z.groups, 1), F32))
+    sizes[...] = jnp.broadcast_to(held[:, :, None], sizes.shape)
     most_ref[...] = jnp.max(held, axis=0, keepdims=True).astype(jnp.int32)
 
     for part in range(z.ny):
@@ -279,15 +281,6 @@
         in_copy("in_t", t_ref, xin_t, k, source, on_y(k)).wait_recv()
         sort_from(source, xin_t, z.cols)
 
-    def cross_to_other(i, _):
-        now = [TOGETHER * i + n for n in range(TOGETHER)]
-        distances_cross([other * hg + n for n in now])
-        for n in now:
-            core_copy("core_c", dc_ref, rc_c, n, other * hg + n).start()
-        return 0
-
-    lax.fori_loop(0, hg // TOGETHER, cross_to_other, 0)
-
     def a1_copy(k, source):
         return copy("a1", dc_ref.at[c * hg + on_x(k)], r1a.at[source], k, source, at(xx=on_x(k)))
 
@@ -296,6 +289,9 @@
 
     def mine(k, _):
         now = (on_x(k), z.nx + on_y(k))
+        distances_cross([other * hg + i for i in now])
+        for i in now:
+            core_copy("core_c", dc_ref, rc_c, i, other * hg + i).start()
         distances_cross([c * hg + i for i in now])
         for i in now:
             core_copy("core_c", dc_ref, rc_c, i, c * hg + i).wait_recv()
@@ -407,7 +403,7 @@
     sub = (1 - way) * y + way * x
     group = c * hg + way * z.nx + member
     block = sub * z.half + lax.rem(zc, z.half)
-    size = jnp.sum(jnp.where(gr_ref[...] == group, 1.0, 0.0), axis=1, keepdims=True)
+    size = sizes[group]
     row_at = (block * 8 + lax.broadcasted_iota(jnp.int32, (8, z.cap), 0)).astype(F32)
     col_at = lax.broadcasted_iota(jnp.int32, (8, z.cap), 1).astype(F32)
     mask = jnp.where((row_at < size) & (col_at < size), 1.0, 0.0)
@@ -490,8 +486,7 @@
             weights = jnp.concatenate([to_self, to_cross], axis=1).astype(BF16)
             values = xs[g]
             pulled = values[0:z.cap].astype(F32) * pulls + jnp.dot(weights, values, preferred_element_type=F32)
-            size_of = jnp.sum(jnp.where(gr_ref[...] == g, 1.0, 0.0), axis=1, keepdims=True)
-            force = pulled / size_of
+            force = pulled / sizes[g]
             high = force.astype(BF16)
             low = (force - high.astype(F32)).astype(BF16)
             found.append((loss, high, low))
@@ -529,10 +524,9 @@
         k = lax.rem(step + z.ny // 2 - 1, z.ny - 1) + 1
         force = unsorted(k)
         top = jnp.maximum(jnp.max(jnp.abs(force), axis=1, keepdims=True), 1e-33)
-        qs[k] = jnp.round(force * (32767.0 / top)).astype(jnp.int32).astype(jnp.int16)
-        unit = top / 32767.0
+        qs[k] = jnp.round(force * (STEPS / top)).astype(jnp.int32).astype(jnp.int16)
         for part in range(parts):
-            spread = jnp.where(same, unit[part * z.lanes:(part + 1) * z.lanes], 0.0)
+            spread = jnp.where(same, top[part * z.lanes:(part + 1) * z.lanes], 0.0)
             scales[k, part:part + 1, :] = jnp.sum(spread, axis=0, keepdims=True)
         for one in out_copies(k, y):
             one.start()
@@ -540,16 +534,23 @@
 
     scales[...] = jnp.zeros_like(scales)
     lax.fori_loop(0, z.ny - 1, send_out, 0)
-    f_ref[:, own_cols] = unsorted(0)
+    def leave(source):
+        cols = pl.ds(pl.multiple_of(source * z.cols, z.cols), z.cols)
+        return pltpu.make_async_copy(fo.at[source], f_ref.at[:, cols], sems.at[ids["own"][0] + 2 + source])
+
+    fo[y] = unsorted(0) * STEPS
+    leave(y).start()
     for k in order:
         source = on_y(z.ny - k)
         for one in out_copies(k, source):
             one.wait_recv()
-        cols = pl.ds(pl.multiple_of(source * z.cols, z.cols), z.cols)
         for part in range(parts):
             rows = slice(part * z.lanes, (part + 1) * z.lanes)
             unit = jnp.sum(jnp.where(same, landed[source, part:part + 1, :], 0.0), axis=1, keepdims=True)
-            f_ref[rows, cols] = ql[source, rows, :].astype(jnp.int32).astype(F32) * unit
+            fo[source, rows, :] = ql[source, rows, :].astype(jnp.int32).astype(F32) * unit
+        leave(source).start()
+    for source in range(z.ny):
+        leave(source).wait()
 
     for k in range(1, z.ny):
         pending += out_copies(k, y)
@@ -566,7 +567,7 @@
         out_shape=(jax.ShapeDtypeStruct((z.rows, z.tile), F32), jax.ShapeDtypeStruct((1, 1), F32),
                    jax.ShapeDtypeStruct((1, 1), jnp.int32)),
         in_specs=[anywhere, anywhere, vmem, smem, smem],
-        out_specs=(vmem, vmem, vmem),
+        out_specs=(anywhere, vmem, vmem),
         scratch_shapes=[
             pltpu.VMEM((z.ny, z.rows, z.cols), BF16),
             pltpu.VMEM((z.ny, z.rows, z.cols), BF16),
@@ -598,10 +599,12 @@
             pltpu.VMEM((1, z.samples), jnp.int32),
             pltpu.VMEM((1, z.samples), jnp.int32),
             pltpu.VMEM((z.samples, 1), jnp.int32),
+            pltpu.VMEM((z.groups, 1, 1), F32),
             pltpu.VMEM((z.groups, 1, z.cap), F32),
             pltpu.VMEM((slots, 2 * z.cols), BF16),
             pltpu.VMEM((z.ny, z.rows, z.cols), jnp.int16),
             pltpu.VMEM((z.ny, z.rows, z.cols), jnp.int16),
+            pltpu.VMEM((z.ny, z.rows, z.cols), F32),
             pltpu.VMEM((z.ny, 8, z.lanes), F32),
             pltpu.VMEM((z.ny, 8, z.lanes), F32),
             pltpu.SemaphoreType.DMA((count,)),
@@ -651,17 +654,19 @@
     pulled = row_wide * pull
     pulled = pulled + jnp.dot(weight_self, students, preferred_element_type=F32)
     pulled = pulled - jnp.dot(weight_cross, teachers, preferred_element_type=F32)
-    return pulled / sizes, loss
+    return pulled / sizes * STEPS, loss
 
 
 def build(mesh, z):
     def step(student, teacher, bw_table, bw_index, group_ids):
         force, loss, largest = sorted_path(z, student, teacher, bw_table, bw_index, group_ids)
-        return lax.cond(
+        force, loss = lax.cond(
             largest <= z.most,
             lambda *held: held[:2],
             lambda *held: dense_path(z, *held[2:]),
             force, loss, student, teacher, bw_table, bw_index, group_ids)
+        force, loss = lax.optimization_barrier((force, loss))
+        return force * (1.0 / STEPS), loss
 
     return jax.shard_map(
         step, mesh=mesh,

time: 89 us -> 90.6 us (1.018)
  other arithmetic: 0 us -> 2.81 us
  local copies, waits for them, and re-layouts: 2.73 us -> 0 us
  Pallas kernels: 82.9 us -> 84.4 us
    mul x0 -> x1, other arithmetic: none -> 2.81 us  [step(): return (force * (1.0 / STEPS), loss)]
    unnamed x1 -> x0, local copies, waits for them, and re-layouts: 2.73 us -> none
    pallas_call x1, Pallas kernels: 82.9 us -> 84.4 us  [sorted_path(): pl.pallas_call(functools.partial(fused, z, ids), out_shape=(jax.ShapeDtyp...]
where the time goes in v6:
time: 90.6 us; the launch traced here: 90.4 us
  Pallas kernels  84.4 us (93%)
  other arithmetic  2.81 us (3%)
  between operations  2.33 us (3%)
    pallas_call x1, Pallas kernels, sorted_path(): pl.pallas_call(functools.partial(fused, z, ids), out_shape=(jax.ShapeDtyp...  84.4 us
    mul x1, other arithmetic, step(): return (force * (1.0 / STEPS), loss)  2.81 us

profile of v6, /device:TPU:1, one launch (start us, length us, event | category | flops | bytes accessed | tf_op | source)
XLA Modules:
  0.0 90.4 jit_solution(13960168673335266521)
XLA Ops:
  0.6 84.4 %grouped.1 = (f32[384,1024]{1,0:T(8,128)}, f32[1,1]{1,0:T(1,128)}, s32[1,1]{1,0:T(1,128)}) custom-call(bf16[384,1024]{1,0:T(8,128)(2,1)} %s_ref.1, bf16[384,1024]{1,0:T(8,128)(2,1)} %t_ref.1, s32[1536]{0:T(1024)} %g_ref.1, f32[8]{0:T(128)} %tab_ref.1, s32[4]{0:T(128)} %idx_ref.1), custom_call_target="tpu_custom_call" | custom-call | tf_op jit(solution)/shard_map/grouped/pallas_call | solution.py:565
  85.6 0.9 conditional.1
  86.5 2.8 %broadcast_multiply_fusion = f32[384,1024]{1,0:T(8,128)} fusion(f32[384,1024]{1,0:T(8,128)} %get-tuple-element.29), kind=kLoop, calls=%fused_computation.48 | loop fusion | flops 393216 | bytes 3145728 | tf_op jit(solution)/shard_map/mul | solution.py:669

commit v7 on v5

--- a/solution.py
+++ b/solution.py
@@ -69,14 +69,14 @@
     sizes = {
         "in_s": z.ny, "in_t": z.ny, "core_s": z.groups // 2, "core_c": z.groups // 2, "s1a": z.nx, "s1b": z.nx, "s2a": z.ny, "s2b": z.ny, "s3": z.nz,
         "a1": z.nx, "b1": z.ny, "a2": z.ny, "b2": z.nx, "z3": z.nz,
-        "gz": z.nz, "g2a": z.ny, "g2b": z.nx, "g1a": z.nx, "g1b": z.ny, "gc": 2, "out": z.ny, "scale": z.ny, "own": 3,
+        "gz": z.nz, "g2a": z.ny, "g2b": z.nx, "g1a": z.nx, "g1b": z.ny, "gc": 2, "out": z.ny, "scale": z.ny, "own": 2,
     }
     return {name: pool.pair(count) for name, count in sizes.items()}, pool.total
 
 
 def fused(z, ids, s_ref, t_ref, g_ref, tab_ref, idx_ref, f_ref, l_ref, most_ref,
           xin_s, xin_t, sort_ref, back_ref, xacc, xs, norms, ds_ref, dc_ref, rc_s, rc_c, r1sa, r1sb, r2sa, r2sb, sum_sa, sum_sb,
-          us_ref, r3s, r1a, r1b, sums, r2a, r2b, u_ref, r3, wf, gr_ref, row_place, col_place, losses, fs, qs, ql, scales, landed, sems):
+          us_ref, r3s, r1a, r1b, sums, r2a, r2b, u_ref, r3, wf, gr_ref, row_place, col_place, sizes, losses, fs, qs, ql, scales, landed, sems):
     y, v = lax.axis_index("pair"), lax.axis_index("value")
     c = lax.rem(v, z.nc)
     x = lax.rem(v // z.nc, z.nx)
@@ -154,6 +154,7 @@
         return seen + jnp.sum(hit, axis=1, keepdims=True)
 
     held = lax.fori_loop(0, z.samples // z.cap, find_places, jnp.zeros((z.groups, 1), F32))
+    sizes[...] = jnp.broadcast_to(held[:, :, None], sizes.shape)
     most_ref[...] = jnp.max(held, axis=0, keepdims=True).astype(jnp.int32)
 
     for part in range(z.ny):
@@ -407,7 +408,7 @@
     sub = (1 - way) * y + way * x
     group = c * hg + way * z.nx + member
     block = sub * z.half + lax.rem(zc, z.half)
-    size = jnp.sum(jnp.where(gr_ref[...] == group, 1.0, 0.0), axis=1, keepdims=True)
+    size = sizes[group]
     row_at = (block * 8 + lax.broadcasted_iota(jnp.int32, (8, z.cap), 0)).astype(F32)
     col_at = lax.broadcasted_iota(jnp.int32, (8, z.cap), 1).astype(F32)
     mask = jnp.where((row_at < size) & (col_at < size), 1.0, 0.0)
@@ -490,8 +491,7 @@
             weights = jnp.concatenate([to_self, to_cross], axis=1).astype(BF16)
             values = xs[g]
             pulled = values[0:z.cap].astype(F32) * pulls + jnp.dot(weights, values, preferred_element_type=F32)
-            size_of = jnp.sum(jnp.where(gr_ref[...] == g, 1.0, 0.0), axis=1, keepdims=True)
-            force = pulled / size_of
+            force = pulled / sizes[g]
             high = force.astype(BF16)
             low = (force - high.astype(F32)).astype(BF16)
             found.append((loss, high, low))
@@ -563,7 +563,7 @@
     vmem, smem, anywhere = (pl.BlockSpec(memory_space=m) for m in (pltpu.VMEM, pltpu.SMEM, pl.ANY))
     force, loss, largest = pl.pallas_call(
         functools.partial(fused, z, ids),
-        out_shape=(jax.ShapeDtypeStruct((z.rows, z.tile), F32), jax.ShapeDtypeStruct((1, 1), F32),
+        out_shape=(pltpu.VMEM((z.rows, z.tile), F32), jax.ShapeDtypeStruct((1, 1), F32),
                    jax.ShapeDtypeStruct((1, 1), jnp.int32)),
         in_specs=[anywhere, anywhere, vmem, smem, smem],
         out_specs=(vmem, vmem, vmem),
@@ -598,6 +598,7 @@
             pltpu.VMEM((1, z.samples), jnp.int32),
             pltpu.VMEM((1, z.samples), jnp.int32),
             pltpu.VMEM((z.samples, 1), jnp.int32),
+            pltpu.VMEM((z.groups, 1, 1), F32),
             pltpu.VMEM((z.groups, 1, z.cap), F32),
             pltpu.VMEM((slots, 2 * z.cols), BF16),
             pltpu.VMEM((z.ny, z.rows, z.cols), jnp.int16),

time: 89 us -> 86.9 us (0.976)
  local copies, waits for them, and re-layouts: 2.73 us -> 1.15 us
    unnamed x1, local copies, waits for them, and re-layouts: 2.73 us -> 1.15 us
where the time goes in v7:
time: 86.9 us; the launch traced here: 86.8 us
  Pallas kernels  82.3 us (95%)
  between operations  2.46 us (3%)
  local copies, waits for them, and re-layouts  1.15 us (1%)
  loops' own time  0.87 us (1%)
    pallas_call x1, Pallas kernels, sorted_path(): pl.pallas_call(functools.partial(fused, z, ids), out_shape=(pltpu.VMEM((z...  82.3 us

profile of v7, /device:TPU:1, one launch (start us, length us, event | category | flops | bytes accessed | tf_op | source)
XLA Modules:
  0.0 86.8 jit_solution(7991816540691978699)
XLA Ops:
  0.6 82.3 %grouped.1 = (f32[384,1024]{1,0:T(8,128)S(1)}, f32[1,1]{1,0:T(1,128)}, s32[1,1]{1,0:T(1,128)}) custom-call(bf16[384,1024]{1,0:T(8,128)(2,1)} %s_ref.1, bf16[384,1024]{1,0:T(8,128)(2,1)} %t_ref.1, s32[1536]{0:T(1024)} %g_ref.1, f32[8]{0:T(128)} %tab_ref.1, s32[4]{0:T(128)} %idx_ref.1), custom_call_target="tpu_custom_call" | custom-call | tf_op jit(solution)/shard_map/grouped/pallas_call | solution.py:564
  83.6 0.9 conditional.1
  84.5 1.1 %copy.25 = f32[384,1024]{1,0:T(8,128)} copy(f32[384,1024]{1,0:T(8,128)S(1)} %get-tuple-element.60) | data formatting | bytes 3145728

commit v8 on v7

--- a/solution.py
+++ b/solution.py
@@ -174,6 +174,7 @@
     own_s.wait()
     own_t.wait()
     xacc[...] = jnp.zeros_like(xacc)
+    scales[...] = jnp.zeros_like(scales)
     tall_rows = slots // 4
 
     def sort_from(source, values, first_col):
@@ -510,8 +511,6 @@
         gc_copy(way_of, other).wait_recv()
         forces(other * hg + way_of * z.nx)
 
-    l_ref[...] = jnp.sum(jnp.sum(losses[...], axis=0), axis=1, keepdims=True) / z.samples
-
     def out_copies(k, source):
         return (copy("out", qs.at[k], ql.at[source], k, source, at(yy=on_y(k))),
                 copy("scale", scales.at[k], landed.at[source], k, source, at(yy=on_y(k))))
@@ -538,9 +537,10 @@
             one.start()
         return 0
 
-    scales[...] = jnp.zeros_like(scales)
     lax.fori_loop(0, z.ny - 1, send_out, 0)
     f_ref[:, own_cols] = unsorted(0)
+    l_ref[...] = jnp.sum(jnp.sum(losses[...], axis=0), axis=1, keepdims=True) / z.samples
+    drain()
     for k in order:
         source = on_y(z.ny - k)
         for one in out_copies(k, source):
@@ -552,8 +552,8 @@
             f_ref[rows, cols] = ql[source, rows, :].astype(jnp.int32).astype(F32) * unit
 
     for k in range(1, z.ny):
-        pending += out_copies(k, y)
-    drain()
+        for one in out_copies(k, y):
+            one.wait_send()
 
 
 def sorted_path(z, student, teacher, bw_table, bw_index, group_ids):

time: 86.9 us -> 86.8 us (level)
  no operation moved by 1% of the time
where the time goes in v8:
time: 86.8 us; the launch traced here: 86.6 us
  Pallas kernels  82.2 us (95%)
  between operations  2.46 us (3%)
  local copies, waits for them, and re-layouts  1.15 us (1%)
  loops' own time  0.87 us (1%)
    pallas_call x1, Pallas kernels, sorted_path(): pl.pallas_call(functools.partial(fused, z, ids), out_shape=(pltpu.VMEM((z...  82.2 us

profile of v8, /device:TPU:1, one launch (start us, length us, event | category | flops | bytes accessed | tf_op | source)
XLA Modules:
  0.0 86.6 jit_solution(8445900864614807656)
XLA Ops:
  0.6 82.2 %grouped.1 = (f32[384,1024]{1,0:T(8,128)S(1)}, f32[1,1]{1,0:T(1,128)}, s32[1,1]{1,0:T(1,128)}) custom-call(bf16[384,1024]{1,0:T(8,128)(2,1)} %s_ref.1, bf16[384,1024]{1,0:T(8,128)(2,1)} %t_ref.1, s32[1536]{0:T(1024)} %g_ref.1, f32[8]{0:T(128)} %tab_ref.1, s32[4]{0:T(128)} %idx_ref.1), custom_call_target="tpu_custom_call" | custom-call | tf_op jit(solution)/shard_map/grouped/pallas_call | solution.py:564
  83.5 0.9 conditional.1
  84.3 1.1 %copy.25 = f32[384,1024]{1,0:T(8,128)} copy(f32[384,1024]{1,0:T(8,128)S(1)} %get-tuple-element.60) | data formatting | bytes 3145728

commit v9 on v8

--- a/solution.py
+++ b/solution.py
@@ -69,7 +69,7 @@
     sizes = {
         "in_s": z.ny, "in_t": z.ny, "core_s": z.groups // 2, "core_c": z.groups // 2, "s1a": z.nx, "s1b": z.nx, "s2a": z.ny, "s2b": z.ny, "s3": z.nz,
         "a1": z.nx, "b1": z.ny, "a2": z.ny, "b2": z.nx, "z3": z.nz,
-        "gz": z.nz, "g2a": z.ny, "g2b": z.nx, "g1a": z.nx, "g1b": z.ny, "gc": 2, "out": z.ny, "scale": z.ny, "own": 2,
+        "gz": z.nz, "g2a": z.ny, "g2b": z.nx, "g1a": z.nx, "g1b": z.ny, "gc": z.groups // 2, "out": z.ny, "scale": z.ny, "own": 2,
     }
     return {name: pool.pair(count) for name, count in sizes.items()}, pool.total
 
@@ -463,22 +463,16 @@
 
     for k in range(1, z.ny):
         g2a_copy(k, on_y(z.ny - k)).wait_recv()
-    for k in range(1, z.nx):
+    for k in order:
         start(g1a_copy(k, x))
     for k in range(1, z.nx):
         g2b_copy(k, on_x(z.nx - k)).wait_recv()
-    for k in range(1, z.ny):
+    for k in order:
         start(g1b_copy(k, y))
-    def gc_copy(way_of, core):
-        place = wf.at[pl.ds(core * hg + way_of * z.nx, z.nx)]
-        return copy("gc", place, place, way_of, way_of, at(cc=other))
-
-    for k in range(1, z.nx):
-        g1a_copy(k, on_x(z.nx - k)).wait_recv()
-    start(gc_copy(0, c))
-    for k in range(1, z.ny):
-        g1b_copy(k, on_y(z.ny - k)).wait_recv()
-    start(gc_copy(1, c))
+
+    def gc_copy(i, core):
+        place = wf.at[core * hg + i]
+        return copy("gc", place, place, i, i, at(cc=other))
 
     last = lax.broadcasted_iota(jnp.int32, (z.cap, z.cap), 1) >= z.most
 
@@ -502,14 +496,19 @@
             fs[rows, 0:z.cols] = high
             fs[rows, z.cols:2 * z.cols] = low
 
-    def forces(first):
-        force_of([first + n for n in range(z.nx)])
-
-    forces(c * hg)
-    forces(c * hg + z.nx)
-    for way_of in range(2):
-        gc_copy(way_of, other).wait_recv()
-        forces(other * hg + way_of * z.nx)
+    for k in [0] + order:
+        now = (on_x(z.nx - k), z.nx + on_y(z.ny - k))
+        if k:
+            g1a_copy(k, now[0]).wait_recv()
+            g1b_copy(k, now[1] - z.nx).wait_recv()
+        for i in now:
+            start(gc_copy(i, c))
+        force_of([c * hg + i for i in now])
+    for k in [0] + order:
+        now = (on_x(z.nx - k), z.nx + on_y(z.ny - k))
+        for i in now:
+            gc_copy(i, other).wait_recv()
+        force_of([other * hg + i for i in now])
 
     def out_copies(k, source):
         return (copy("out", qs.at[k], ql.at[source], k, source, at(yy=on_y(k))),

time: 86.8 us -> 86.8 us (level)
  no operation moved by 1% of the time
where the time goes in v9:
time: 86.8 us; the launch traced here: 86.6 us
  Pallas kernels  82.1 us (95%)
  between operations  2.46 us (3%)
  local copies, waits for them, and re-layouts  1.15 us (1%)
  loops' own time  0.87 us (1%)
    pallas_call x1, Pallas kernels, sorted_path(): pl.pallas_call(functools.partial(fused, z, ids), out_shape=(pltpu.VMEM((z...  82.1 us

profile of v9, /device:TPU:1, one launch (start us, length us, event | category | flops | bytes accessed | tf_op | source)
XLA Modules:
  0.0 86.6 jit_solution(10933875968698427771)
XLA Ops:
  0.6 82.1 %grouped.1 = (f32[384,1024]{1,0:T(8,128)S(1)}, f32[1,1]{1,0:T(1,128)}, s32[1,1]{1,0:T(1,128)}) custom-call(bf16[384,1024]{1,0:T(8,128)(2,1)} %s_ref.1, bf16[384,1024]{1,0:T(8,128)(2,1)} %t_ref.1, s32[1536]{0:T(1024)} %g_ref.1, f32[8]{0:T(128)} %tab_ref.1, s32[4]{0:T(128)} %idx_ref.1), custom_call_target="tpu_custom_call" | custom-call | tf_op jit(solution)/shard_map/grouped/pallas_call | solution.py:563
  83.5 0.9 conditional.1
  84.3 1.1 %copy.25 = f32[384,1024]{1,0:T(8,128)} copy(f32[384,1024]{1,0:T(8,128)S(1)} %get-tuple-element.60) | data formatting | bytes 3145728

commit v10 on v9

--- a/solution.py
+++ b/solution.py
@@ -11,7 +11,7 @@
 F32, BF16 = jnp.float32, jnp.bfloat16
 
 
-TOGETHER = 4
+TOGETHER = 8
 
 
 class Sizes:

time: 86.8 us -> 86.2 us (level)
  no operation moved by 1% of the time
where the time goes in v10:
time: 86.2 us; the launch traced here: 86.1 us
  Pallas kernels  81.6 us (95%)
  between operations  2.46 us (3%)
  local copies, waits for them, and re-layouts  1.15 us (1%)
  loops' own time  0.87 us (1%)
    pallas_call x1, Pallas kernels, sorted_path(): pl.pallas_call(functools.partial(fused, z, ids), out_shape=(pltpu.VMEM((z...  81.6 us

profile of v10, /device:TPU:1, one launch (start us, length us, event | category | flops | bytes accessed | tf_op | source)
XLA Modules:
  0.0 86.1 jit_solution(8892292090474757095)
XLA Ops:
  0.6 81.6 %grouped.1 = (f32[384,1024]{1,0:T(8,128)S(1)}, f32[1,1]{1,0:T(1,128)}, s32[1,1]{1,0:T(1,128)}) custom-call(bf16[384,1024]{1,0:T(8,128)(2,1)} %s_ref.1, bf16[384,1024]{1,0:T(8,128)(2,1)} %t_ref.1, s32[1536]{0:T(1024)} %g_ref.1, f32[8]{0:T(128)} %tab_ref.1, s32[4]{0:T(128)} %idx_ref.1), custom_call_target="tpu_custom_call" | custom-call | tf_op jit(solution)/shard_map/grouped/pallas_call | solution.py:563
  82.9 0.9 %conditional.1 = (f32[384,1024]{1,0:T(8,128)S(1)}, f32[]{:T(128)}) conditional(s32[]{:T(128)} %bitcast.17, (bf16[384,1024]{1,0:T(8,128)(2,1)}, s32[1536]{0:T(1024)}, bf16[384,1024]{1,0:T(8,128)(2,1)}, s32[4]{0:T(128)}, f32[8]{0:T(128)}) %tuple.16, (f32[1,1]{1,0:T(1,128)}, f32[384,1024]{1,0:T(8,128)S(1)}) %tuple.35), branch_computations={%region_0.8_spmd, %region_8.9_spmd} | conditional | flops 4906549248 | bytes 332803776 | solution.py:660
  83.8 1.1 %copy.25 = f32[384,1024]{1,0:T(8,128)} copy(f32[384,1024]{1,0:T(8,128)S(1)} %get-tuple-element.60) | data formatting | bytes 3145728

commit v11 on v10

--- a/solution.py
+++ b/solution.py
@@ -296,21 +296,19 @@
     def b1_copy(k, source):
         return copy("b1", dc_ref.at[c * hg + z.nx + on_y(k)], r1b.at[source], k, source, at(yy=on_y(k)))
 
-    def mine(k, _):
+    def mine(k):
         now = (on_x(k), z.nx + on_y(k))
         distances_cross([c * hg + i for i in now])
         for i in now:
             core_copy("core_c", dc_ref, rc_c, i, c * hg + i).wait_recv()
             dc_ref[c * hg + i] += rc_c[i]
 
-        @pl.when(k < z.nx)
-        def _():
+        if k < z.nx:
             a1_copy(k, x).start()
             b1_copy(k, y).start()
 
-        return 0
-
-    lax.fori_loop(1, z.nx + 1, mine, 0)
+    for k in range(1, z.nx + 1):
+        mine(k)
     for i in range(hg):
         pending.append(core_copy("core_c", dc_ref, rc_c, i, other * hg + i))
     for k in range(1, z.nx):

time: 86.2 us -> 86.2 us (level)
  no operation moved by 1% of the time
where the time goes in v11:
time: 86.2 us; the launch traced here: 86.1 us
  Pallas kernels  81.6 us (95%)
  between operations  2.46 us (3%)
  local copies, waits for them, and re-layouts  1.15 us (1%)
  loops' own time  0.87 us (1%)
    pallas_call x1, Pallas kernels, sorted_path(): pl.pallas_call(functools.partial(fused, z, ids), out_shape=(pltpu.VMEM((z...  81.6 us

profile of v11, /device:TPU:1, one launch (start us, length us, event | category | flops | bytes accessed | tf_op | source)
XLA Modules:
  0.0 86.1 jit_solution(1356244376562092531)
XLA Ops:
  0.6 81.6 %grouped.1 = (f32[384,1024]{1,0:T(8,128)S(1)}, f32[1,1]{1,0:T(1,128)}, s32[1,1]{1,0:T(1,128)}) custom-call(bf16[384,1024]{1,0:T(8,128)(2,1)} %s_ref.1, bf16[384,1024]{1,0:T(8,128)(2,1)} %t_ref.1, s32[1536]{0:T(1024)} %g_ref.1, f32[8]{0:T(128)} %tab_ref.1, s32[4]{0:T(128)} %idx_ref.1), custom_call_target="tpu_custom_call" | custom-call | tf_op jit(solution)/shard_map/grouped/pallas_call | solution.py:561
  82.9 0.9 %conditional.1 = (f32[384,1024]{1,0:T(8,128)S(1)}, f32[]{:T(128)}) conditional(s32[]{:T(128)} %bitcast.17, (bf16[384,1024]{1,0:T(8,128)(2,1)}, s32[1536]{0:T(1024)}, bf16[384,1024]{1,0:T(8,128)(2,1)}, s32[4]{0:T(128)}, f32[8]{0:T(128)}) %tuple.16, (f32[1,1]{1,0:T(1,128)}, f32[384,1024]{1,0:T(8,128)S(1)}) %tuple.35), branch_computations={%region_0.8_spmd, %region_8.9_spmd} | conditional | flops 4906549248 | bytes 332803776 | solution.py:658
  83.8 1.1 %copy.25 = f32[384,1024]{1,0:T(8,128)} copy(f32[384,1024]{1,0:T(8,128)S(1)} %get-tuple-element.60) | data formatting | bytes 3145728
